TPU v7x, 128 devices: a whole 4x4x4 slice. The times are simulated.
128 devices in a mesh: lat: 4 (over z), lon: 32 (over x, y, core).
Axes of the slice: x: 4, y: 4, z: 4, core: 2. Of those that a mesh axis runs over, the one named last changes fastest.
Arguments:
- grid_lat: bfloat16 [131072, 512], P(('lat', 'lon')), may hold values from -6 to 6
- mesh_lat: bfloat16 [8192, 512], P(('lat', 'lon')), may hold values from -6 to 6
- g2m_send: int32 [128, 9, 256], P(('lat', 'lon')), may hold values from -1 to 1023, as said below
- g2m_recv: int32 [128, 9, 256], P(('lat', 'lon')), may hold values from -1 to 63, as said below
- g2m_feat: bfloat16 [128, 4, 2304], P(('lat', 'lon')), may hold values from -6 to 6
- halo_lists: int32 [128, 4, 16], P(('lat', 'lon')), may hold values from 0 to 63
- proc_send: int32 [128, 512], P(('lat', 'lon')), may hold values from 0 to 127, as said below
- proc_recv: int32 [128, 512], P(('lat', 'lon')), may hold values from 0 to 63
- cotangent: bfloat16 [8192, 512], P(('lat', 'lon')), may hold values from -6 to 6
- w_grid_send: bfloat16 [512, 512], replicated, may hold values from -0.25 to 0.25
- w_grid_recv: bfloat16 [512, 512], replicated, may hold values from -0.25 to 0.25
- w_grid_feat: bfloat16 [4, 512], replicated, may hold values from -3 to 3
- w_grid_out: bfloat16 [512, 512], replicated, may hold values from -0.25 to 0.25
- gain_grid: float32 [512], replicated, may hold values from 0.5 to 1.5
- w_node_in: bfloat16 [1024, 512], replicated, may hold values from -0.1875 to 0.1875
- w_node_out: bfloat16 [512, 512], replicated, may hold values from -0.25 to 0.25
- gain_node: float32 [512], replicated, may hold values from 0.5 to 1.5
- w_proc_send: bfloat16 [512, 512], replicated, may hold values from -0.25 to 0.25
- w_proc_recv: bfloat16 [512, 512], replicated, may hold values from -0.25 to 0.25
- w_proc_out: bfloat16 [512, 512], replicated, may hold values from -0.25 to 0.25
- gain_proc: float32 [512], replicated, may hold values from 0.5 to 1.5
- w_upd_in: bfloat16 [1024, 512], replicated, may hold values from -0.1875 to 0.1875
- w_upd_out: bfloat16 [512, 512], replicated, may hold values from -0.25 to 0.25
- gain_upd: float32 [512], replicated, may hold values from 0.5 to 1.5
Outputs:
- mesh_out: float32 [8192, 512], P(('lat', 'lon'))
- grid_grad: float32 [131072, 512], P(('lat', 'lon'))
- grad_grid_send: float32 [512, 512], replicated
- grad_grid_recv: float32 [512, 512], replicated
- grad_grid_out: float32 [512, 512], replicated
- grad_proc_send: float32 [512, 512], replicated
- grad_proc_recv: float32 [512, 512], replicated
- grad_proc_out: float32 [512, 512], replicated
Inputs may be any that keep to these rules, and one draw needn't show every extreme that they name: `g2m_send`: row within source device s's 1024 grid rows of the sender of slot c from s to the owner (a + dlat, (b + dlon) mod 32) at offset k, or -1 for an unused slot. Slot (s, k, c) is used exactly when the owner's g2m_recv[o, k, c] is; offsets that leave the lat range are never used; in every draw some owner's slots are full from every source that exists. `g2m_recv`: row within owner o's 64 mesh rows of the receiver of slot c from the source at offset k below o, or -1 for an unused slot. `proc_send`: row of device p's sender table: own rows first, then the blocks from lat below, lat above, lon below, lon above. Devices at lat index 0 never name the block from below, those at the last lat index never the block from above.
All inputs are finite; a program needn't handle non-finite values.
Results may differ from a plain program's by a relative error of at most 0.018.
Values may be sent and summed in bfloat16 or wider, within the bound.
A program may use at most 128 MiB of HBM per device.

v0:
```python
import jax
import jax.numpy as jnp
from jax import lax
from jax.sharding import PartitionSpec as P

EPSILON = 1e-05
product_precision = lax.Precision.DEFAULT


def passed_along(value, axis, steps):
    count = lax.axis_size(axis)
    first, last = (max(0, -steps), min(count, count - steps))
    return lax.ppermute(value, axis, [(source, source + steps) for source in range(first, last)])


def passed_along_2(block, axis, distance):
    devices = range(lax.axis_size(axis))
    route = [((i - distance) % len(devices), i) for i in devices]
    return lax.ppermute(block, axis, route)


def inner_rows(matrix_one, matrix_two, precision=None):
    return lax.dot_general(
        matrix_one,
        matrix_two,
        (((0,), (0,)), ((), ())),
        precision=precision,
        preferred_element_type=jnp.float32,
    )


def outer_cols(matrix_one, matrix_two):
    return lax.dot_general(
        matrix_one, matrix_two, (((1,), (1,)), ((), ())), preferred_element_type=jnp.float32
    )


def tail_forward(preact, weight_out, gain_vec):
    sigmoid_act = jax.nn.sigmoid(preact)
    hidden = (preact * sigmoid_act).astype(jnp.bfloat16)
    mixed_out = jnp.dot(hidden, weight_out, preferred_element_type=jnp.float32)
    centre = mixed_out - jnp.mean(mixed_out, axis=-1, keepdims=True)
    inv_std = lax.rsqrt(jnp.mean(centre * centre, axis=-1, keepdims=True) + EPSILON)
    normed = centre * inv_std
    return (normed * gain_vec, (sigmoid_act, hidden, normed, inv_std))


def tail_backward(preact, stash, grad_out, weight_out, gain_vec):
    sigmoid_act, hidden, normed, inv_std = stash
    upstream = grad_out * gain_vec
    grad_mixed = inv_std * (
        upstream
        - jnp.mean(upstream, axis=-1, keepdims=True)
        - normed * jnp.mean(upstream * normed, axis=-1, keepdims=True)
    )
    grad_mixed = grad_mixed.astype(jnp.bfloat16)
    weight_grad = inner_rows(hidden, grad_mixed)
    grad_hidden = outer_cols(grad_mixed, weight_out)
    slope = sigmoid_act + preact * sigmoid_act * (1.0 - sigmoid_act)
    return (grad_hidden * slope, weight_grad)


def tiles_lat(block, shift_by):
    return passed_along(block, "lat", shift_by)


def tiles_lon(block, shift_by):
    return passed_along_2(block, "lon", shift_by)


def grads_lat(block, shift_by):
    return passed_along(block, "lat", shift_by)


def grads_lon(block, shift_by):
    return passed_along_2(block, "lon", shift_by)


def send_terms(slots):
    blocks = slots.reshape((3, 3) + slots.shape[1:])
    rows = jnp.stack([tiles_lat(blocks[0], -1), blocks[1], tiles_lat(blocks[2], 1)], axis=0)
    moved = jnp.stack([tiles_lon(rows[:, 0], -1), rows[:, 1], tiles_lon(rows[:, 2], 1)], axis=1)
    return moved.reshape(slots.shape)


def send_grads(slots):
    blocks = slots.reshape((3, 3) + slots.shape[1:])
    cols = jnp.stack(
        [grads_lon(blocks[:, 0], 1), blocks[:, 1], grads_lon(blocks[:, 2], -1)], axis=1
    )
    moved = jnp.stack([grads_lat(cols[0], 1), cols[1], grads_lat(cols[2], -1)], axis=0)
    return moved.reshape(slots.shape)


def along_lat(block, shift_by):
    return passed_along(block, "lat", shift_by)


def along_lon(block, shift_by):
    return passed_along_2(block, "lon", shift_by)


def return_lat(block, shift_by):
    return passed_along(block, "lat", shift_by)


def return_lon(block, shift_by):
    return passed_along_2(block, "lon", shift_by)


def local(
    grid_lat,
    mesh_lat,
    g2m_send,
    g2m_recv,
    g2m_feat,
    halo_lists,
    proc_send,
    proc_recv,
    cotangent,
    w_grid_send,
    w_grid_recv,
    w_grid_feat,
    w_grid_out,
    gain_grid,
    w_node_in,
    w_node_out,
    gain_node,
    w_proc_send,
    w_proc_recv,
    w_proc_out,
    gain_proc,
    w_upd_in,
    w_upd_out,
    gain_upd,
):
    width = mesh_lat.shape[1]
    grid_count = grid_lat.shape[0]
    mesh_count = mesh_lat.shape[0]
    senders = g2m_send[0]
    offset_count, capacity = senders.shape
    sender_ok = senders >= 0
    sender_idx = jnp.maximum(senders, 0).reshape(-1)
    grid_terms = jnp.dot(grid_lat, w_grid_send, preferred_element_type=jnp.float32)
    picked = jnp.take(grid_terms, sender_idx, axis=0).reshape(offset_count, capacity, width)
    slots = jnp.where(sender_ok[:, :, None], picked, 0.0).astype(jnp.bfloat16)
    arrived = send_terms(slots).reshape(offset_count * capacity, width)
    receivers = g2m_recv[0].reshape(-1)
    recv_ok = (receivers >= 0).astype(jnp.float32)
    recv_idx = jnp.maximum(receivers, 0)
    mesh_ids = jnp.arange(mesh_count, dtype=jnp.int32)
    onehot_grid = (receivers[:, None] == mesh_ids[None, :]).astype(jnp.float32)
    recv_terms = jnp.dot(mesh_lat, w_grid_recv, preferred_element_type=jnp.float32)
    edge_terms = inner_rows(g2m_feat[0], w_grid_feat)
    grid_pre = arrived.astype(jnp.float32) + jnp.take(recv_terms, recv_idx, axis=0) + edge_terms
    message, grid_stash = tail_forward(grid_pre, w_grid_out, gain_grid)
    message = message * recv_ok[:, None]
    grid_sum = inner_rows(onehot_grid, message, product_precision)
    node_in = jnp.concatenate([mesh_lat, grid_sum.astype(jnp.bfloat16)], axis=1)
    node_pre = jnp.dot(node_in, w_node_in, preferred_element_type=jnp.float32)
    node_upd, node_stash = tail_forward(node_pre, w_node_out, gain_node)
    state_one = mesh_lat.astype(jnp.float32) + node_upd
    state_bf = state_one.astype(jnp.bfloat16)
    proc_terms = jnp.dot(state_bf, w_proc_send, preferred_element_type=jnp.float32).astype(
        jnp.bfloat16
    )
    proc_recv_terms = jnp.dot(state_bf, w_proc_recv, preferred_element_type=jnp.float32)
    halo_rows = halo_lists[0]
    halo_count = halo_rows.shape[1]
    outgoing = jnp.take(proc_terms, halo_rows.reshape(-1), axis=0).reshape(4, halo_count, width)
    incoming = [
        along_lat(outgoing[0], 1),
        along_lat(outgoing[1], -1),
        along_lon(outgoing[2], 1),
        along_lon(outgoing[3], -1),
    ]
    sender_table = jnp.concatenate([proc_terms] + incoming, axis=0)
    edge_from = proc_send[0]
    edge_to = proc_recv[0]
    table_ids = jnp.arange(sender_table.shape[0], dtype=jnp.int32)
    onehot_from = (edge_from[:, None] == table_ids[None, :]).astype(jnp.float32)
    onehot_to = (edge_to[:, None] == mesh_ids[None, :]).astype(jnp.float32)
    proc_pre = jnp.take(sender_table, edge_from, axis=0).astype(jnp.float32) + jnp.take(
        proc_recv_terms, edge_to, axis=0
    )
    proc_msg, proc_stash = tail_forward(proc_pre, w_proc_out, gain_proc)
    proc_sum = inner_rows(onehot_to, proc_msg, product_precision)
    upd_in = jnp.concatenate([state_bf, proc_sum.astype(jnp.bfloat16)], axis=1)
    upd_pre = jnp.dot(upd_in, w_upd_in, preferred_element_type=jnp.float32)
    upd_out, upd_stash = tail_forward(upd_pre, w_upd_out, gain_upd)
    mesh_out = state_one + upd_out
    grad_top = cotangent.astype(jnp.float32)
    grad_upd_pre, unused_upd = tail_backward(upd_pre, upd_stash, grad_top, w_upd_out, gain_upd)
    grad_upd_in = outer_cols(grad_upd_pre.astype(jnp.bfloat16), w_upd_in)
    grad_state = grad_top + grad_upd_in[:, :width]
    grad_proc_msg = jnp.dot(onehot_to, grad_upd_in[:, width:])
    grad_proc_pre, grad_proc_out = tail_backward(
        proc_pre, proc_stash, grad_proc_msg, w_proc_out, gain_proc
    )
    grad_table = inner_rows(onehot_from, grad_proc_pre, product_precision)
    grad_recv2 = inner_rows(onehot_to, grad_proc_pre, product_precision)
    grad_halo = grad_table[mesh_count:].astype(jnp.bfloat16).reshape(4, halo_count, width)
    returned = jnp.stack(
        [
            return_lat(grad_halo[0], -1),
            return_lat(grad_halo[1], 1),
            return_lon(grad_halo[2], -1),
            return_lon(grad_halo[3], 1),
        ],
        axis=0,
    )
    returned = returned.reshape(4 * halo_count, width).astype(jnp.float32)
    onehot_halo = (halo_rows.reshape(-1)[:, None] == mesh_ids[None, :]).astype(jnp.float32)
    grad_terms = grad_table[:mesh_count] + inner_rows(onehot_halo, returned, product_precision)
    grad_terms_bf = grad_terms.astype(jnp.bfloat16)
    grad_recv2_bf = grad_recv2.astype(jnp.bfloat16)
    grad_proc_send = inner_rows(state_bf, grad_terms_bf)
    grad_proc_recv = inner_rows(state_bf, grad_recv2_bf)
    grad_state = (
        grad_state + outer_cols(grad_terms_bf, w_proc_send) + outer_cols(grad_recv2_bf, w_proc_recv)
    )
    grad_node_pre, unused_node = tail_backward(
        node_pre, node_stash, grad_state, w_node_out, gain_node
    )
    grad_grid_sum = outer_cols(grad_node_pre.astype(jnp.bfloat16), w_node_in[width:])
    grad_message = jnp.dot(onehot_grid, grad_grid_sum)
    grad_grid_pre, grad_grid_out = tail_backward(
        grid_pre, grid_stash, grad_message, w_grid_out, gain_grid
    )
    grad_recv_terms = inner_rows(onehot_grid, grad_grid_pre, product_precision)
    grad_grid_recv = inner_rows(mesh_lat, grad_recv_terms.astype(jnp.bfloat16))
    slot_grads = grad_grid_pre.astype(jnp.bfloat16).reshape(offset_count, capacity, width)
    back_slots = send_grads(slot_grads).astype(jnp.float32)
    back_slots = jnp.where(sender_ok[:, :, None], back_slots, 0.0).reshape(
        offset_count * capacity, width
    )
    grad_grid_terms = jax.ops.segment_sum(back_slots, sender_idx, num_segments=grid_count)
    grad_grid_bf = grad_grid_terms.astype(jnp.bfloat16)
    grad_grid_send = inner_rows(grid_lat, grad_grid_bf)
    grid_grad = outer_cols(grad_grid_bf, w_grid_send)
    summed = lax.psum(
        (
            grad_grid_send,
            grad_grid_recv,
            grad_grid_out,
            grad_proc_send,
            grad_proc_recv,
            grad_proc_out,
        ),
        ("lat", "lon"),
    )
    return (mesh_out, grid_grad) + tuple(summed)


def solution(mesh):
    placed = (
        P(("lat", "lon"), None),
        P(("lat", "lon"), None),
        P(("lat", "lon"), None, None),
        P(("lat", "lon"), None, None),
        P(("lat", "lon"), None, None),
        P(("lat", "lon"), None, None),
        P(("lat", "lon"), None),
        P(("lat", "lon"), None),
        P(("lat", "lon"), None),
        P(),
        P(),
        P(),
        P(),
        P(),
        P(),
        P(),
        P(),
        P(),
        P(),
        P(),
        P(),
        P(),
        P(),
        P(),
    )
    return jax.shard_map(
        local,
        mesh=mesh,
        in_specs=placed,
        out_specs=(P(("lat", "lon"), None), P(("lat", "lon"), None), P(), P(), P(), P(), P(), P()),
        check_vma=False,
    )
```

profile of v0, /device:TPU:1, one launch (start us, length us, event | category | flops | bytes accessed | tf_op | source)
XLA Modules:
  0.0 380.1 jit_solution(4527027398960618478)
XLA Ops:
  8.0 1.3 fusion.105
  10.0 1.7 fusion.120
  11.7 7.5 %gather_fusion = bf16[2304,512]{1,0:T(8,128)(2,1)} fusion(bf16[1024,512]{1,0:T(8,128)(2,1)S(1)} %fusion.120, s32[3072]{0:T(1024)S(1)} %pad_clamp_fusion.1), kind=kCustom, calls=%fused_computation | custom fusion | bytes 4727808 | tf_op jit(solution)/shard_map/jit(_take)/gather | solution.py:145
  19.3 2.9 select_convert_fusion
  23.3 5.3 %collective-permute-start.1 = (bf16[3,256,512]{2,1,0:T(8,128)(2,1)}, bf16[3,256,512]{2,1,0:T(8,128)(2,1)}, u32[]{:S(2)}, u32[]{:S(2)}) collective-permute-start(bf16[3,256,512]{2,1,0:T(8,128)(2,1)} %get-tuple-element.50), channel_id=1, source_target_pairs={{0,32},{32,64},{64,96},{1,33},{33,65},{65,97},{2,34},{34,66},{66,9... | collective-permute-start | bytes 2359304 | tf_op jit(solution)/shard_map/ppermute | solution.py:13
  30.3 13.9 %collective-permute-done.1 = bf16[3,256,512]{2,1,0:T(8,128)(2,1)} collective-permute-done((bf16[3,256,512]{2,1,0:T(8,128)(2,1)}, bf16[3,256,512]{2,1,0:T(8,128)(2,1)}, u32[]{:S(2)}, u32[]{:S(2)}) %collective-permute-start.1) | collective-permute-done | bytes 786464 | tf_op jit(solution)/shard_map/ppermute | solution.py:13
  44.2 4.5 %collective-permute-done = bf16[3,256,512]{2,1,0:T(8,128)(2,1)} collective-permute-done((bf16[3,256,512]{2,1,0:T(8,128)(2,1)S(1)}, bf16[3,256,512]{2,1,0:T(8,128)(2,1)}, u32[]{:S(2)}, u32[]{:S(2)}) %collective-permute-start) | collective-permute-done | bytes 786464 | tf_op jit(solution)/shard_map/ppermute | solution.py:13
  48.7 1.6 pad_maximum_fusion
  51.4 3.0 collective-permute-start.3
  54.5 6.9 %gather_fusion.1 = f32[2304,512]{1,0:T(8,128)} fusion(f32[64,512]{1,0:T(8,128)S(1)} %fusion.121, s32[3072]{0:T(1024)S(1)} %pad_clamp_fusion), kind=kCustom, calls=%fused_computation.1 | custom fusion | bytes 9446400 | tf_op jit(solution)/shard_map/jit(_take)/gather | solution.py:155
  61.5 2.1 collective-permute-done.3
  63.6 2.6 collective-permute-done.2
  66.2 1.8 pad_maximum_fusion.1
  69.0 3.9 %fusion.5 = (bf16[2304,512]{1,0:T(8,128)(2,1)S(1)}, f32[2304,512]{1,0:T(8,128)}) fusion(bf16[4,512]{1,0:T(4,128)(2,1)S(1)} %copy-done.78, bf16[1,4,2304]{2,1,0:T(4,128)(2,1)S(1)} %copy-done.77, f32[2304,512]{1,0:T(8,128)S(1)} %copy-done.3, pred[2304]{0:T(1024)(128)(4,1)S(1)} %get-tuple-element.62, bf16[2304,512]{1,0:T(8,128)(2,1)S(1)} %bitcast.119), kind=kOutput, calls=%fused_computation.22 | convolution fusion | flops 20054016 | bytes 14180608 | tf_op jit(solution)/shard_map/dot_general | solution.py:23
  72.9 1.5 fusion.113
  75.0 1.6 copy-done.1
  76.6 1.5 fusion.20
  80.1 2.6 collective-permute-start.4
  83.0 1.3 collective-permute-start.5
  84.6 2.4 collective-permute-start.7
  87.0 1.6 gather_fusion.4
  88.7 2.0 gather_fusion.3
  96.3 2.5 fusion.24
  98.8 1.5 fusion.107
  103.0 4.7 %collective-permute-start.10 = (bf16[16,512]{1,0:T(8,128)(2,1)S(1)}, bf16[16,512]{1,0:T(8,128)(2,1)S(1)}, u32[]{:S(2)}, u32[]{:S(2)}) collective-permute-start(bf16[16,512]{1,0:T(8,128)(2,1)S(1)} %get-tuple-element.55), channel_id=1, source_target_pairs={{1,0},{2,1},{3,2},{4,3},{5,4},{6,5},{7,6},{8,7},{9,8},{10,9},{11,1... | collective-permute-start | bytes 49160 | tf_op jit(solution)/shard_map/ppermute | solution.py:19
  107.7 4.3 %collective-permute-start.9 = (bf16[16,512]{1,0:T(8,128)(2,1)S(1)}, bf16[16,512]{1,0:T(8,128)(2,1)S(1)}, u32[]{:S(2)}, u32[]{:S(2)}) collective-permute-start(bf16[16,512]{1,0:T(8,128)(2,1)S(1)} %get-tuple-element.56), channel_id=1, source_target_pairs={{0,32},{32,64},{64,96},{1,33},{33,65},{65,97},{2,34},{34,66},{66,9... | collective-permute-start | bytes 49160 | tf_op jit(solution)/shard_map/ppermute | solution.py:13
  112.0 1.5 collective-permute-start.8
  113.9 2.6 collective-permute-done.8
  117.9 6.3 %fusion.106 = (f32[2304]{0:T(1024)S(1)}, f32[2304]{0:T(1024)S(1)}, f32[2304,512]{0,1:T(8,128)}) fusion(f32[2304]{0:T(1024)} %copy-done.42, f32[2304,512]{0,1:T(8,128)} %copy-done.1, f32[2304]{0:T(1024)S(1)} %broadcast_multiply_fusion.2, f32[512]{0:T(512)S(1)} %copy-done.67, bf16[64,512]{1,0:T(8,128)(2,1)S(1)} %fusion.18, ...), kind=kOutput, calls=%fused_computation.200 | convolution fusion | flops 191770112 | bytes 10078208 | tf_op jit(solution)/shard_map/dot_general | solution.py:226
  124.3 4.8 %multiply_convert_fusion = bf16[2304,512]{0,1:T(8,128)(2,1)S(1)} fusion(f32[2304,512]{0,1:T(8,128)} %get-tuple-element.82, f32[2304,512]{0,1:T(8,128)} %copy-done.1, f32[2304]{0:T(1024)S(1)} %broadcast_multiply_fusion, f32[2304]{0:T(1024)S(1)} %broadcast_multiply_fusion.1, f32[2304]{0:T(1024)S(1)} %copy-done.43, f32[2304]{0:T(1024)S(1)} %broadcast_multiply_fusion.2), kind=kLoop, calls=%fused_computation.12 | loop fusion | flops 8257536 | bytes 11833344 | tf_op jit(solution)/shard_map/convert_element_type | solution.py:56
  129.1 6.0 %convolution_multiply_fusion = bf16[2304,512]{1,0:T(8,128)(2,1)S(1)} fusion(bf16[2304,512]{0,1:T(8,128)(2,1)S(1)} %multiply_convert_fusion, bf16[512,512]{1,0:T(8,128)(2,1)S(1)} %copy-done.34, f32[2304,512]{1,0:T(8,128)} %get-tuple-element.67), kind=kOutput, calls=%fused_computation.6 | convolution fusion | flops 1218576384 | bytes 9961472 | tf_op jit(solution)/shard_map/dot_general | solution.py:33
  135.2 1.4 slice_bitcast_fusion.5
  136.6 6.4 %collective-permute-start.13 = (bf16[3,256,512]{2,1,0:T(8,128)(2,1)}, bf16[3,256,512]{2,1,0:T(8,128)(2,1)}, u32[]{:S(2)}, u32[]{:S(2)}) collective-permute-start(bf16[3,256,512]{2,1,0:T(8,128)(2,1)} %get-tuple-element.44), channel_id=1, source_target_pairs={{1,0},{2,1},{3,2},{4,3},{5,4},{6,5},{7,6},{8,7},{9,8},{10,9},{11,1... | collective-permute-start | bytes 2359304 | tf_op jit(solution)/shard_map/ppermute | solution.py:19
  143.1 2.2 fusion.125
  145.2 2.7 fusion.126
  148.3 3.9 %collective-permute-done.12 = bf16[3,256,512]{2,1,0:T(8,128)(2,1)} collective-permute-done((bf16[3,256,512]{2,1,0:T(8,128)(2,1)}, bf16[3,256,512]{2,1,0:T(8,128)(2,1)}, u32[]{:S(2)}, u32[]{:S(2)}) %collective-permute-start.12) | collective-permute-done | bytes 786464 | tf_op jit(solution)/shard_map/ppermute | solution.py:19
  152.3 1.6 pad_maximum_fusion.2
  153.9 1.5 slice_bitcast_fusion.2
  156.7 4.9 %collective-permute-start.14 = (bf16[3,256,512]{2,1,0:T(8,128)(2,1)}, bf16[3,256,512]{2,1,0:T(8,128)(2,1)}, u32[]{:S(2)}, u32[]{:S(2)}) collective-permute-start(bf16[3,256,512]{2,1,0:T(8,128)(2,1)} %get-tuple-element.40), channel_id=1, source_target_pairs={{0,32},{32,64},{64,96},{1,33},{33,65},{65,97},{2,34},{34,66},{66,9... | collective-permute-start | bytes 2359304 | tf_op jit(solution)/shard_map/ppermute | solution.py:13
  162.9 2.1 convolution_bitcast_fusion
  165.0 4.9 %fusion.123 = f32[512,512]{1,0:T(8,128)} fusion(bf16[2304,512]{1,0:T(8,128)(2,1)} %copy-done.2, bf16[2304,512]{0,1:T(8,128)(2,1)} %copy-done.12), kind=kOutput, calls=%fused_computation.215 | convolution fusion | flops 1207959552 | bytes 5767168 | tf_op jit(solution)/shard_map/dot_general | solution.py:23
  171.8 3.0 pad_maximum_fusion.3
  174.8 21.1 %scatter_custom_fusion = f32[1024,512]{1,0:T(8,128)S(1)} fusion(s32[2304]{0:T(1024)} %copy-done.47, bf16[2304,512]{1,0:T(8,128)(2,1)} %bitcast.116, f32[]{:T(128)} %constant.97.clone.1, pred[2304]{0:T(1024)(128)(4,1)S(1)} %ge.68), kind=kCustom, calls=%fused_computation.10 | custom fusion | flops 3538944 | bytes 4459776 | tf_op jit(solution)/shard_map/scatter-add | solution.py:237
  196.0 1.7 convolution_bitcast_fusion.1
  197.7 3.1 fusion.35
  200.8 163.3 %all-reduce.3.cloned.1.call-done = (f32[512,512]{0,1:T(8,128)}, f32[512,512]{0,1:T(8,128)}, f32[512,512]{1,0:T(8,128)}, f32[512,512]{1,0:T(8,128)}, f32[512,512]{1,0:T(8,128)}, /*index=5*/f32[512,512]{1,0:T(8,128)}) async-done(((f32[512,512]{0,1:T(8,128)}, f32[512,512]{0,1:T(8,128)}, f32[512,512]{1,0:T(8,128)}, f32[512,512]{1,0:T(8,128)}, f32[512,512]{1,0:T(8,128)}, /*index=5*/f32[512,512]{1,0:T(8,128)}), ...) | async-done | bytes 6291472 | tf_op jit(solution)/shard_map/psum | solution.py:241
  364.1 2.6 copy.50
  366.7 2.6 copy.51
  (250 shorter events, 27.8 us)
Async XLA Ops:
  7.2 356.9 %all-reduce.3.cloned.1.call-start = ((), (), s32[]{:S(2)}) async-start(), calls=%async_computation | async-start | bytes 12582912 | tf_op jit(solution)/shard_map/psum | solution.py:241
  22.1 7.7 %copy-start.55 = (s32[1,9,256]{2,0,1:T(1,128)S(1)}, s32[1,9,256]{2,0,1:T(1,128)}, u32[]{:S(2)}) copy-start(s32[1,9,256]{2,0,1:T(1,128)} %param.27) | copy-start | bytes 27652
  22.2 7.8 %copy-start.56 = (s32[1,4,16]{2,1,0:T(4,128)S(1)}, s32[1,4,16]{2,1,0:T(4,128)}, u32[]{:S(2)}) copy-start(s32[1,4,16]{2,1,0:T(4,128)} %param.29) | copy-start | bytes 772
  22.2 7.9 %copy-start.44 = (s32[1,512]{1,0:T(1,128)S(1)}, s32[1,512]{1,0:T(1,128)}, u32[]{:S(2)}) copy-start(s32[1,512]{1,0:T(1,128)} %param.31) | copy-start | bytes 6148
  22.2 7.9 %copy-start.52 = (s32[1,512]{1,0:T(1,128)S(1)}, s32[1,512]{1,0:T(1,128)}, u32[]{:S(2)}) copy-start(s32[1,512]{1,0:T(1,128)} %param.30) | copy-start | bytes 6148
  22.2 7.9 %copy-start.20 = (bf16[64,512]{1,0:T(8,128)(2,1)S(1)}, bf16[64,512]{1,0:T(8,128)(2,1)}, u32[]{:S(2)}) copy-start(bf16[64,512]{1,0:T(8,128)(2,1)} %param.25) | copy-start | bytes 196612
  22.2 7.9 %copy-start.36 = (bf16[512,512]{1,0:T(8,128)(2,1)S(1)}, bf16[512,512]{1,0:T(8,128)(2,1)}, u32[]{:S(2)}) copy-start(bf16[512,512]{1,0:T(8,128)(2,1)} %param.34) | copy-start | bytes 1572868
  23.3 20.9 %collective-permute-start.1 = (bf16[3,256,512]{2,1,0:T(8,128)(2,1)}, bf16[3,256,512]{2,1,0:T(8,128)(2,1)}, u32[]{:S(2)}, u32[]{:S(2)}) collective-permute-start(bf16[3,256,512]{2,1,0:T(8,128)(2,1)} %get-tuple-element.50), channel_id=1, source_target_pairs={{0,32},{32,64},{64,96},{1,33},{33,65},{65,97},{2,34},{34,66},{66,9... | collective-permute-start | bytes 2359304 | tf_op jit(solution)/shard_map/ppermute | solution.py:13
  28.6 20.1 %collective-permute-start = (bf16[3,256,512]{2,1,0:T(8,128)(2,1)S(1)}, bf16[3,256,512]{2,1,0:T(8,128)(2,1)}, u32[]{:S(2)}, u32[]{:S(2)}) collective-permute-start(bf16[3,256,512]{2,1,0:T(8,128)(2,1)S(1)} %get-tuple-element.49), channel_id=1, source_target_pairs={{32,0},{64,32},{96,64},{33,1},{65,33},{97,65},{34,2},{66,34},{98,6... | collective-permute-start | bytes 2359304 | tf_op jit(solution)/shard_map/ppermute | solution.py:13
  51.4 12.2 %collective-permute-start.3 = (bf16[3,256,512]{2,1,0:T(8,128)(2,1)}, bf16[3,256,512]{2,1,0:T(8,128)(2,1)}, u32[]{:S(2)}, u32[]{:S(2)}) collective-permute-start(bf16[3,256,512]{2,1,0:T(8,128)(2,1)} %get-tuple-element.47), channel_id=1, source_target_pairs={{31,0},{0,1},{1,2},{2,3},{3,4},{4,5},{5,6},{6,7},{7,8},{8,9},{9,10... | collective-permute-start | bytes 2359304 | tf_op jit(solution)/shard_map/ppermute | solution.py:19
  54.4 11.8 %collective-permute-start.2 = (bf16[3,256,512]{2,1,0:T(8,128)(2,1)S(1)}, bf16[3,256,512]{2,1,0:T(8,128)(2,1)}, u32[]{:S(2)}, u32[]{:S(2)}) collective-permute-start(bf16[3,256,512]{2,1,0:T(8,128)(2,1)S(1)} %get-tuple-element.46), channel_id=1, source_target_pairs={{1,0},{2,1},{3,2},{4,3},{5,4},{6,5},{7,6},{8,7},{9,8},{10,9},{11,1... | collective-permute-start | bytes 2359304 | tf_op jit(solution)/shard_map/ppermute | solution.py:19
  54.5 20.5 %copy-start.38 = (s32[2304]{0:T(1024)}, s32[2304]{0:T(1024)S(1)}, u32[]{:S(2)}) copy-start(s32[2304]{0:T(1024)S(1)} %eq.56) | copy-start | bytes 27652
  54.5 13.5 %copy-start.77 = (bf16[1,4,2304]{2,1,0:T(4,128)(2,1)S(1)}, bf16[1,4,2304]{2,1,0:T(4,128)(2,1)}, u32[]{:S(2)}) copy-start(bf16[1,4,2304]{2,1,0:T(4,128)(2,1)} %param.28) | copy-start | bytes 55300
  54.5 13.5 %copy-start.78 = (bf16[4,512]{1,0:T(4,128)(2,1)S(1)}, bf16[4,512]{1,0:T(4,128)(2,1)}, u32[]{:S(2)}) copy-start(bf16[4,512]{1,0:T(4,128)(2,1)} %param.35) | copy-start | bytes 12292
  61.5 29.2 %copy-start.70 = (pred[512]{0:T(512)(128)(4,1)}, pred[512]{0:T(512)(128)(4,1)S(1)}, u32[]{:S(2)}) copy-start(pred[512]{0:T(512)(128)(4,1)S(1)} %get-tuple-element.87) | copy-start | bytes 1540
  61.5 29.2 %copy-start.72 = (pred[512]{0:T(512)(128)(4,1)}, pred[512]{0:T(512)(128)(4,1)S(1)}, u32[]{:S(2)}) copy-start(pred[512]{0:T(512)(128)(4,1)S(1)} %get-tuple-element.88) | copy-start | bytes 1540
  78.7 9.9 %copy-start.57 = (f32[64]{0:T(128)}, f32[64]{0:T(128)S(1)}, u32[]{:S(2)}) copy-start(f32[64]{0:T(128)S(1)} %broadcast_multiply_fusion.11) | copy-start | bytes 772
  78.9 9.7 %copy-start.62 = (f32[64]{0:T(128)}, f32[64]{0:T(128)S(1)}, u32[]{:S(2)}) copy-start(f32[64]{0:T(128)S(1)} %add_rsqrt_fusion.3) | copy-start | bytes 772
  80.1 8.5 %collective-permute-start.4 = (bf16[16,512]{1,0:T(8,128)(2,1)S(1)}, bf16[16,512]{1,0:T(8,128)(2,1)S(1)}, u32[]{:S(2)}, u32[]{:S(2)}) collective-permute-start(bf16[16,512]{1,0:T(8,128)(2,1)S(1)} %get-tuple-element.60), channel_id=1, source_target_pairs={{0,32},{32,64},{64,96},{1,33},{33,65},{65,97},{2,34},{34,66},{66,9... | collective-permute-start | bytes 49160 | tf_op jit(solution)/shard_map/ppermute | solution.py:13
  83.0 5.6 %collective-permute-start.5 = (bf16[16,512]{1,0:T(8,128)(2,1)S(1)}, bf16[16,512]{1,0:T(8,128)(2,1)S(1)}, u32[]{:S(2)}, u32[]{:S(2)}) collective-permute-start(bf16[16,512]{1,0:T(8,128)(2,1)S(1)} %get-tuple-element.59), channel_id=1, source_target_pairs={{32,0},{64,32},{96,64},{33,1},{65,33},{97,65},{34,2},{66,34},{98,6... | collective-permute-start | bytes 49160 | tf_op jit(solution)/shard_map/ppermute | solution.py:13
  84.3 4.4 %collective-permute-start.6 = (bf16[16,512]{1,0:T(8,128)(2,1)S(1)}, bf16[16,512]{1,0:T(8,128)(2,1)S(1)}, u32[]{:S(2)}, u32[]{:S(2)}) collective-permute-start(bf16[16,512]{1,0:T(8,128)(2,1)S(1)} %get-tuple-element.58), channel_id=1, source_target_pairs={{31,0},{0,1},{1,2},{2,3},{3,4},{4,5},{5,6},{6,7},{7,8},{8,9},{9,10... | collective-permute-start | bytes 49160 | tf_op jit(solution)/shard_map/ppermute | solution.py:19
  84.6 4.1 %collective-permute-start.7 = (bf16[16,512]{1,0:T(8,128)(2,1)S(1)}, bf16[16,512]{1,0:T(8,128)(2,1)S(1)}, u32[]{:S(2)}, u32[]{:S(2)}) collective-permute-start(bf16[16,512]{1,0:T(8,128)(2,1)S(1)} %get-tuple-element.57), channel_id=1, source_target_pairs={{1,0},{2,1},{3,2},{4,3},{5,4},{6,5},{7,6},{8,7},{9,8},{10,9},{11,1... | collective-permute-start | bytes 49160 | tf_op jit(solution)/shard_map/ppermute | solution.py:19
  101.4 12.2 %copy-start.46 = (s32[1,512]{1,0:T(1,128)S(1)}, s32[1,512]{1,0:T(1,128)}, u32[]{:S(2)}) copy-start(s32[1,512]{1,0:T(1,128)} %param.31) | copy-start | bytes 6148
  101.4 15.1 %copy-start.69 = (s32[64]{0:T(128)S(1)}, s32[64]{0:T(128)}, u32[]{:S(2)}) copy-start(s32[64]{0:T(128)} %copy-done.68) | copy-start | bytes 772
  101.4 15.4 %copy-start.14 = (bf16[512,512]{1,0:T(8,128)(2,1)S(1)}, bf16[512,512]{1,0:T(8,128)(2,1)}, u32[]{:S(2)}) copy-start(bf16[512,512]{1,0:T(8,128)(2,1)} %param.41) | copy-start | bytes 1572868
  101.4 15.4 %copy-start.21 = (f32[64,1024]{1,0:T(8,128)S(1)}, f32[64,1024]{1,0:T(8,128)}, u32[]{:S(2)}) copy-start(f32[64,1024]{1,0:T(8,128)} %fusion.24) | copy-start | bytes 786436
  101.4 15.4 %copy-start.29 = (bf16[64,512]{1,0:T(8,128)(2,1)S(1)}, bf16[64,512]{1,0:T(8,128)(2,1)}, u32[]{:S(2)}) copy-start(bf16[64,512]{1,0:T(8,128)(2,1)} %param.32) | copy-start | bytes 196612
  102.3 14.8 %copy-start.16 = (bf16[512,512]{1,0:T(8,128)(2,1)S(1)}, bf16[512,512]{1,0:T(8,128)(2,1)}, u32[]{:S(2)}) copy-start(bf16[512,512]{1,0:T(8,128)(2,1)} %param.42) | copy-start | bytes 1572868
  102.3 14.8 %copy-start.51 = (f32[512]{0:T(512)S(1)}, f32[512]{0:T(512)}, u32[]{:S(2)}) copy-start(f32[512]{0:T(512)} %param.40) | copy-start | bytes 6148
  102.3 14.8 %copy-start.59 = (f32[64]{0:T(128)S(1)}, f32[64]{0:T(128)}, u32[]{:S(2)}) copy-start(f32[64]{0:T(128)} %copy-done.57) | copy-start | bytes 772
  102.3 14.8 %copy-start.64 = (f32[64]{0:T(128)S(1)}, f32[64]{0:T(128)}, u32[]{:S(2)}) copy-start(f32[64]{0:T(128)} %copy-done.62) | copy-start | bytes 772
  102.4 15.2 %copy-start.41 = (f32[64,512]{1,0:T(8,128)S(1)}, f32[64,512]{1,0:T(8,128)}, u32[]{:S(2)}) copy-start(f32[64,512]{1,0:T(8,128)} %copy-done.40) | copy-start | bytes 393220
  102.4 15.2 %copy-start.76 = (bf16[512,512]{1,0:T(8,128)(2,1)S(1)}, bf16[512,512]{1,0:T(8,128)(2,1)}, u32[]{:S(2)}) copy-start(bf16[512,512]{1,0:T(8,128)(2,1)} %param.39) | copy-start | bytes 1572868
  102.7 15.2 %copy-start.11 = (bf16[1024,512]{1,0:T(8,128)(2,1)S(1)}, bf16[1024,512]{1,0:T(8,128)(2,1)}, u32[]{:S(2)}) copy-start(bf16[1024,512]{1,0:T(8,128)(2,1)} %param.38) | copy-start | bytes 3145732
  102.8 15.1 %copy-start.67 = (f32[512]{0:T(512)S(1)}, f32[512]{0:T(512)}, u32[]{:S(2)}) copy-start(f32[512]{0:T(512)} %param.37) | copy-start | bytes 6148
  102.8 11.1 %collective-permute-start.11 = (bf16[16,512]{1,0:T(8,128)(2,1)S(1)}, bf16[16,512]{1,0:T(8,128)(2,1)S(1)}, u32[]{:S(2)}, u32[]{:S(2)}) collective-permute-start(bf16[16,512]{1,0:T(8,128)(2,1)S(1)} %get-tuple-element.54), channel_id=1, source_target_pairs={{31,0},{0,1},{1,2},{2,3},{3,4},{4,5},{5,6},{6,7},{7,8},{8,9},{9,10... | collective-permute-start | bytes 49160 | tf_op jit(solution)/shard_map/ppermute | solution.py:19
  103.0 10.9 %collective-permute-start.10 = (bf16[16,512]{1,0:T(8,128)(2,1)S(1)}, bf16[16,512]{1,0:T(8,128)(2,1)S(1)}, u32[]{:S(2)}, u32[]{:S(2)}) collective-permute-start(bf16[16,512]{1,0:T(8,128)(2,1)S(1)} %get-tuple-element.55), channel_id=1, source_target_pairs={{1,0},{2,1},{3,2},{4,3},{5,4},{6,5},{7,6},{8,7},{9,8},{10,9},{11,1... | collective-permute-start | bytes 49160 | tf_op jit(solution)/shard_map/ppermute | solution.py:19
  107.7 6.2 %collective-permute-start.9 = (bf16[16,512]{1,0:T(8,128)(2,1)S(1)}, bf16[16,512]{1,0:T(8,128)(2,1)S(1)}, u32[]{:S(2)}, u32[]{:S(2)}) collective-permute-start(bf16[16,512]{1,0:T(8,128)(2,1)S(1)} %get-tuple-element.56), channel_id=1, source_target_pairs={{0,32},{32,64},{64,96},{1,33},{33,65},{65,97},{2,34},{34,66},{66,9... | collective-permute-start | bytes 49160 | tf_op jit(solution)/shard_map/ppermute | solution.py:13
  112.0 4.5 %collective-permute-start.8 = (bf16[16,512]{1,0:T(8,128)(2,1)S(1)}, bf16[16,512]{1,0:T(8,128)(2,1)S(1)}, u32[]{:S(2)}, u32[]{:S(2)}) collective-permute-start(bf16[16,512]{1,0:T(8,128)(2,1)S(1)} %get-tuple-element.53), channel_id=1, source_target_pairs={{32,0},{64,32},{96,64},{33,1},{65,33},{97,65},{34,2},{66,34},{98,6... | collective-permute-start | bytes 49160 | tf_op jit(solution)/shard_map/ppermute | solution.py:13
  116.8 7.4 %copy-start.26 = (bf16[64,512]{1,0:T(8,128)(2,1)}, bf16[64,512]{1,0:T(8,128)(2,1)S(1)}, u32[]{:S(2)}) copy-start(bf16[64,512]{1,0:T(8,128)(2,1)S(1)} %fusion.23) | copy-start | bytes 196612
  135.1 7.9 %copy-start.54 = (pred[9,256]{1,0:T(8,128)(4,1)S(1)}, pred[9,256]{1,0:T(8,128)(4,1)}, u32[]{:S(2)}) copy-start(pred[9,256]{1,0:T(8,128)(4,1)} %get-tuple-element.63) | copy-start | bytes 6916
  136.6 11.7 %collective-permute-start.13 = (bf16[3,256,512]{2,1,0:T(8,128)(2,1)}, bf16[3,256,512]{2,1,0:T(8,128)(2,1)}, u32[]{:S(2)}, u32[]{:S(2)}) collective-permute-start(bf16[3,256,512]{2,1,0:T(8,128)(2,1)} %get-tuple-element.44), channel_id=1, source_target_pairs={{1,0},{2,1},{3,2},{4,3},{5,4},{6,5},{7,6},{8,7},{9,8},{10,9},{11,1... | collective-permute-start | bytes 2359304 | tf_op jit(solution)/shard_map/ppermute | solution.py:19
  143.0 9.3 %collective-permute-start.12 = (bf16[3,256,512]{2,1,0:T(8,128)(2,1)}, bf16[3,256,512]{2,1,0:T(8,128)(2,1)}, u32[]{:S(2)}, u32[]{:S(2)}) collective-permute-start(bf16[3,256,512]{2,1,0:T(8,128)(2,1)} %get-tuple-element.43), channel_id=1, source_target_pairs={{31,0},{0,1},{1,2},{2,3},{3,4},{4,5},{5,6},{6,7},{7,8},{8,9},{9,10... | collective-permute-start | bytes 2359304 | tf_op jit(solution)/shard_map/ppermute | solution.py:19
  143.0 9.2 %copy-start.9 = (bf16[3,1,256,512]{3,2,0,1:T(8,128)(2,1)S(1)}, bf16[3,1,256,512]{3,2,0,1:T(8,128)(2,1)}, u32[]{:S(2)}) copy-start(bf16[3,1,256,512]{3,2,0,1:T(8,128)(2,1)} %get-tuple-element.45) | copy-start | bytes 2359300
  153.9 7.7 %copy-start.27 = (bf16[64,512]{1,0:T(8,128)(2,1)S(1)}, bf16[64,512]{1,0:T(8,128)(2,1)}, u32[]{:S(2)}) copy-start(bf16[64,512]{1,0:T(8,128)(2,1)} %copy-done.26) | copy-start | bytes 196612
  153.9 9.0 %copy-start.39 = (s32[2304]{0:T(1024)S(1)}, s32[2304]{0:T(1024)}, u32[]{:S(2)}) copy-start(s32[2304]{0:T(1024)} %copy-done.38) | copy-start | bytes 27652
  155.4 15.5 %collective-permute-start.15 = (bf16[3,256,512]{2,1,0:T(8,128)(2,1)}, bf16[3,256,512]{2,1,0:T(8,128)(2,1)}, u32[]{:S(2)}, u32[]{:S(2)}) collective-permute-start(bf16[3,256,512]{2,1,0:T(8,128)(2,1)} %get-tuple-element.41), channel_id=1, source_target_pairs={{32,0},{64,32},{96,64},{33,1},{65,33},{97,65},{34,2},{66,34},{98,6... | collective-permute-start | bytes 2359304 | tf_op jit(solution)/shard_map/ppermute | solution.py:13
  156.7 15.1 %collective-permute-start.14 = (bf16[3,256,512]{2,1,0:T(8,128)(2,1)}, bf16[3,256,512]{2,1,0:T(8,128)(2,1)}, u32[]{:S(2)}, u32[]{:S(2)}) collective-permute-start(bf16[3,256,512]{2,1,0:T(8,128)(2,1)} %get-tuple-element.40), channel_id=1, source_target_pairs={{0,32},{32,64},{64,96},{1,33},{33,65},{65,97},{2,34},{34,66},{66,9... | collective-permute-start | bytes 2359304 | tf_op jit(solution)/shard_map/ppermute | solution.py:13
  (48 other events, 117.0 us)
Sparse Core Ops, SparseCore 0:
  197.8 166.1 all-reduce.2
where the time goes:
time: 381 us; the launch traced here: 380 us
  waiting for transfers between devices  195 us (51%)
  matrix products  48.3 us (13%)
  other arithmetic  43.8 us (11%)
  starting transfers between devices  39.5 us (10%)
  local copies, waits for them, and re-layouts  37.7 us (10%)
  between operations  15.5 us (4%)
    psum x1, waiting for transfers between devices, local(): lax.psum((grad_grid_send, grad_grid_recv, grad_grid_out, grad_proc_send,...  163 us
    ppermute x8, waiting for transfers between devices, passed_along(): lax.ppermute(value, axis, [(source, source + steps) for source in range(f...  23 us
    ppermute x8, starting transfers between devices, passed_along(): lax.ppermute(value, axis, [(source, source + steps) for source in range(f...  22.4 us
    dot_general x12, matrix products, inner_rows(): lax.dot_general(matrix_one, matrix_two, (((0,), (0,)), ((), ())), precisi...  21.5 us
    scatter-add x1, other arithmetic, local(): jax.ops.segment_sum(back_slots, sender_idx, num_segments=grid_count)  21.1 us
    ppermute x8, starting transfers between devices, passed_along_2(): return lax.ppermute(block, axis, route)  17 us
    unnamed x168, local copies, waits for them, and re-layouts  13.7 us
    dot_general x7, matrix products, outer_cols(): lax.dot_general(matrix_one, matrix_two, (((1,), (1,)), ((), ())), preferr...  13.4 us
  transfers between devices with their start and end apart: 17, of which 10 were waited for; matrix products, arithmetic and copies ran while one was open for 7% of the time, Pallas kernels for 0%

commit v1 on v0

--- a/solution.py
+++ b/solution.py
@@ -1,6 +1,8 @@
 import jax
 import jax.numpy as jnp
 from jax import lax
+from jax.experimental import pallas as pl
+from jax.experimental.pallas import tpu as pltpu
 from jax.sharding import PartitionSpec as P
 
 EPSILON = 1e-05
@@ -106,6 +108,174 @@
 
 def return_lon(block, shift_by):
     return passed_along_2(block, "lon", shift_by)
+
+
+MESH = pl.DeviceIdType.MESH
+ORDERS = ((0, 1, 2), (1, 2, 0), (2, 0, 1))
+
+
+def coordinates():
+    lon = lax.axis_index("lon")
+    return (lax.axis_index("lat"), lon // 8, lax.rem(lon // 2, 4), lax.rem(lon, 2))
+
+
+def device(z, x, y, c):
+    return (z, (x * 4 + y) * 2 + c)
+
+
+def ring_peer(me, dim, step):
+    spot = list(me)
+    spot[dim] = lax.rem(me[dim] + step, 4)
+    return device(*spot)
+
+
+def core_peer(me):
+    return device(me[0], me[1], me[2], 1 - me[3])
+
+
+def greet(peers):
+    barrier = pltpu.get_barrier_semaphore()
+    for peer in peers:
+        pl.semaphore_signal(barrier, inc=1, device_id=peer, device_id_type=MESH)
+    pl.semaphore_wait(barrier, len(peers))
+
+
+class Reduction:
+    def __init__(self, me, order, source, bufs, send, recv):
+        self.me, self.order, self.source = me, ORDERS[order], source
+        self.s0, self.r0, self.s1, self.r1, self.s2, self.r2, self.s3, self.r3, self.full = bufs
+        self.send, self.recv = send, recv
+        self.spot = [me[d] for d in self.order]
+        self.copies = {}
+
+    def start(self, slot, src, dst, peer):
+        copy = pltpu.make_async_remote_copy(
+            src_ref=src, dst_ref=dst, send_sem=self.send.at[slot], recv_sem=self.recv.at[slot],
+            device_id=peer, device_id_type=MESH,
+        )
+        copy.start()
+        self.copies[slot] = copy
+
+    def begin(self):
+        other = pl.multiple_of((1 - self.me[3]) * 256, 256)
+        self.s0[...] = self.source[pl.ds(other, 256), :].astype(jnp.bfloat16)
+        self.start(0, self.s0, self.r0, core_peer(self.me))
+
+    def scatter(self, level):
+        own = self.spot[level]
+        if level == 0:
+            self.copies[0].wait_recv()
+            mine = pl.multiple_of(self.me[3] * 256, 256)
+            total = self.source[pl.ds(mine, 256), :] + self.r0[...].astype(jnp.float32)
+            self.s1[...] = total.astype(jnp.bfloat16).reshape(4, 64, 512)
+            sends, lands, base = self.s1, self.r1, 1
+        elif level == 1:
+            self.arrive(1)
+            total = self.s1[self.spot[0]].astype(jnp.float32)
+            for k in range(3):
+                total = total + self.r1[k].astype(jnp.float32)
+            self.s2[...] = total.astype(jnp.bfloat16).reshape(4, 16, 512)
+            sends, lands, base = self.s2, self.r2, 4
+        else:
+            self.arrive(4)
+            total = self.s2[self.spot[1]].astype(jnp.float32)
+            for k in range(3):
+                total = total + self.r2[k].astype(jnp.float32)
+            total = total.astype(jnp.bfloat16)
+            for j in range(4):
+                self.s3[j] = total[:, j * 128 : (j + 1) * 128]
+            sends, lands, base = self.s3, self.r3, 7
+        for step in (1, 3, 2):
+            goal = lax.rem(own + step, 4)
+            self.start(base + step - 1, sends.at[goal], lands.at[step - 1], ring_peer(self.me, self.order[level], step))
+
+    def arrive(self, base):
+        for k in range(3):
+            self.copies[base + k].wait_recv()
+
+    def place(self, level):
+        spots = (self.me[3], *self.spot)
+        return self.full.at[spots[: level + 1]]
+
+    def gather(self, level):
+        if level == 3:
+            self.arrive(7)
+            total = self.s3[self.spot[2]].astype(jnp.float32)
+            for k in range(3):
+                total = total + self.r3[k].astype(jnp.float32)
+            a, b, c = self.spot
+            self.full[self.me[3], a, b, c] = total.astype(jnp.bfloat16)
+        else:
+            self.arrive(10 + 3 * (2 - level))
+        base = 10 + 3 * (3 - level)
+        block = self.place(level)
+        if level == 0:
+            self.start(19, block, block, core_peer(self.me))
+        else:
+            for step in (1, 3, 2):
+                self.start(base + step - 1, block, block, ring_peer(self.me, self.order[level - 1], step))
+
+    def finish(self):
+        self.copies[19].wait_recv()
+        for copy in self.copies.values():
+            copy.wait_send()
+
+
+def reduction_scratch(count):
+    shapes = ((256, 512), (256, 512), (4, 64, 512), (3, 64, 512), (4, 16, 512), (3, 16, 512), (4, 16, 128), (3, 16, 128))
+    return [pltpu.VMEM((count,) + s, jnp.bfloat16) for s in shapes]
+
+
+def reduce_kernel(*refs):
+    grads, full = refs[:6], refs[6]
+    bufs, send, recv = refs[7:15], refs[15], refs[16]
+    me = coordinates()
+    greet([core_peer(me)] + [ring_peer(me, d, s) for d in range(3) for s in (1, 2, 3)])
+    parts = [
+        Reduction(me, g % 3, grads[g], [b.at[g] for b in bufs] + [full.at[g]], send.at[g], recv.at[g])
+        for g in range(6)
+    ]
+    for part in parts:
+        part.begin()
+    for level in range(3):
+        for part in parts:
+            part.scatter(level)
+    for level in (3, 2, 1, 0):
+        for part in parts:
+            part.gather(level)
+    for part in parts:
+        part.finish()
+
+
+def spread_kernel(full, *outs):
+    for g, out in enumerate(outs):
+        def rows(i, carry):
+            h, rest = i // 16, lax.rem(i, 16)
+            a, b = rest // 4, lax.rem(rest, 4)
+            for c in range(4):
+                out[pl.ds(pl.multiple_of(i * 16, 16), 16), c * 128 : (c + 1) * 128] = full[g, h, a, b, c].astype(jnp.float32)
+            return carry
+        lax.fori_loop(0, 32, rows, 0)
+
+
+def reduced(grads):
+    vmem = pl.BlockSpec(memory_space=pltpu.VMEM)
+    full = pl.pallas_call(
+        reduce_kernel,
+        out_shape=jax.ShapeDtypeStruct((6, 2, 4, 4, 4, 16, 128), jnp.bfloat16),
+        in_specs=[vmem] * 6,
+        out_specs=vmem,
+        scratch_shapes=reduction_scratch(6) + [pltpu.SemaphoreType.DMA((6, 20)), pltpu.SemaphoreType.DMA((6, 20))],
+        compiler_params=pltpu.CompilerParams(collective_id=0, has_side_effects=True, vmem_limit_bytes=60 << 20),
+        name="reduce",
+    )(*grads)
+    return pl.pallas_call(
+        spread_kernel,
+        out_shape=[jax.ShapeDtypeStruct((512, 512), jnp.float32)] * 6,
+        in_specs=[vmem],
+        out_specs=[vmem] * 6,
+        name="spread",
+    )(full)
 
 
 def local(
@@ -238,7 +408,7 @@
     grad_grid_bf = grad_grid_terms.astype(jnp.bfloat16)
     grad_grid_send = inner_rows(grid_lat, grad_grid_bf)
     grid_grad = outer_cols(grad_grid_bf, w_grid_send)
-    summed = lax.psum(
+    summed = reduced(
         (
             grad_grid_send,
             grad_grid_recv,
@@ -246,8 +416,7 @@
             grad_proc_send,
             grad_proc_recv,
             grad_proc_out,
-        ),
-        ("lat", "lon"),
+        )
     )
     return (mesh_out, grid_grad) + tuple(summed)
 

time: 381 us -> 251 us (0.66)
  waiting for transfers between devices: 195 us -> 32 us
  Pallas kernels: 0 us -> 56.2 us
  between operations: 15.5 us -> 2.07 us
  local copies, waits for them, and re-layouts: 37.7 us -> 28.6 us
    psum x1 -> x0, waiting for transfers between devices: 163 us -> none  [local(): lax.psum((grad_grid_send, grad_grid_recv, grad_grid_out, grad_proc_send,...]
    pallas_call x0 -> x2, Pallas kernels: none -> 56.2 us  [the longest x1 48.5 us: reduced(): pl.pallas_call(reduce_kernel, out_shape=jax.ShapeDtypeStruct((6, 2, 4, 4,...]
    unnamed x168 -> x154, local copies, waits for them, and re-layouts: 13.7 us -> 4.57 us
  transfers between devices with their start and end apart: 17 -> 16, of which waited for: 10 -> 9; matrix products, arithmetic and copies ran while one was open for 7% -> 9% of each run, Pallas kernels for 0% -> 0%
where the time goes in v1:
time: 251 us; the launch traced here: 250 us
  Pallas kernels  56.2 us (22%)
  matrix products  48.3 us (19%)
  other arithmetic  43.8 us (17%)
  starting transfers between devices  39.5 us (16%)
  waiting for transfers between devices  32 us (13%)
  local copies, waits for them, and re-layouts  28.6 us (11%)
    pallas_call x1, Pallas kernels, reduced(): pl.pallas_call(reduce_kernel, out_shape=jax.ShapeDtypeStruct((6, 2, 4, 4,...  48.5 us
    ppermute x8, waiting for transfers between devices, passed_along(): lax.ppermute(value, axis, [(source, source + steps) for source in range(f...  23 us
    ppermute x8, starting transfers between devices, passed_along(): lax.ppermute(value, axis, [(source, source + steps) for source in range(f...  22.4 us
    dot_general x12, matrix products, inner_rows(): lax.dot_general(matrix_one, matrix_two, (((0,), (0,)), ((), ())), precisi...  21.5 us
    scatter-add x1, other arithmetic, local(): jax.ops.segment_sum(back_slots, sender_idx, num_segments=grid_count)  21.1 us
    ppermute x8, starting transfers between devices, passed_along_2(): return lax.ppermute(block, axis, route)  17 us
    dot_general x7, matrix products, outer_cols(): lax.dot_general(matrix_one, matrix_two, (((1,), (1,)), ((), ())), preferr...  13.4 us
    ppermute x8, waiting for transfers between devices, passed_along_2(): return lax.ppermute(block, axis, route)  9.02 us
  transfers between devices with their start and end apart: 16, of which 9 were waited for; matrix products, arithmetic and copies ran while one was open for 9% of the time, Pallas kernels for 0%

profile of v1, /device:TPU:1, one launch (start us, length us, event | category | flops | bytes accessed | tf_op | source)
XLA Modules:
  0.0 250.5 jit_solution(11499447120100059853)
XLA Ops:
  1.5 1.3 fusion.105
  3.4 1.7 fusion.120
  5.2 7.5 %gather_fusion = bf16[2304,512]{1,0:T(8,128)(2,1)} fusion(bf16[1024,512]{1,0:T(8,128)(2,1)S(1)} %fusion.120, s32[3072]{0:T(1024)S(1)} %pad_clamp_fusion.1), kind=kCustom, calls=%fused_computation | custom fusion | bytes 4727808 | tf_op jit(solution)/shard_map/jit(_take)/gather | solution.py:315
  12.7 2.9 %select_convert_fusion = bf16[9,256,512]{2,1,0:T(8,128)(2,1)S(1)} fusion(bf16[9,256,512]{2,1,0:T(8,128)(2,1)} %bitcast.118, pred[9,256]{1,0:T(8,128)(4,1)S(1)} %get-tuple-element.75, pred[9,256]{1,0:T(8,128)(4,1)S(1)} %get-tuple-element.76), kind=kLoop, calls=%fused_computation.19 | loop fusion | flops 2359296 | bytes 4723200 | tf_op jit(solution)/shard_map/convert_element_type | solution.py:316
  16.8 5.2 %collective-permute-start.1 = (bf16[3,256,512]{2,1,0:T(8,128)(2,1)}, bf16[3,256,512]{2,1,0:T(8,128)(2,1)}, u32[]{:S(2)}, u32[]{:S(2)}) collective-permute-start(bf16[3,256,512]{2,1,0:T(8,128)(2,1)} %get-tuple-element.40), channel_id=1, source_target_pairs={{0,32},{32,64},{64,96},{1,33},{33,65},{65,97},{2,34},{34,66},{66,9... | collective-permute-start | bytes 2359304 | tf_op jit(solution)/shard_map/ppermute | solution.py:15
  23.8 13.9 %collective-permute-done.1 = bf16[3,256,512]{2,1,0:T(8,128)(2,1)} collective-permute-done((bf16[3,256,512]{2,1,0:T(8,128)(2,1)}, bf16[3,256,512]{2,1,0:T(8,128)(2,1)}, u32[]{:S(2)}, u32[]{:S(2)}) %collective-permute-start.1) | collective-permute-done | bytes 786464 | tf_op jit(solution)/shard_map/ppermute | solution.py:15
  37.6 4.5 %collective-permute-done = bf16[3,256,512]{2,1,0:T(8,128)(2,1)} collective-permute-done((bf16[3,256,512]{2,1,0:T(8,128)(2,1)S(1)}, bf16[3,256,512]{2,1,0:T(8,128)(2,1)}, u32[]{:S(2)}, u32[]{:S(2)}) %collective-permute-start) | collective-permute-done | bytes 786464 | tf_op jit(solution)/shard_map/ppermute | solution.py:15
  42.2 1.6 pad_maximum_fusion
  44.8 3.0 %collective-permute-start.3 = (bf16[3,256,512]{2,1,0:T(8,128)(2,1)}, bf16[3,256,512]{2,1,0:T(8,128)(2,1)}, u32[]{:S(2)}, u32[]{:S(2)}) collective-permute-start(bf16[3,256,512]{2,1,0:T(8,128)(2,1)} %get-tuple-element.37), channel_id=1, source_target_pairs={{31,0},{0,1},{1,2},{2,3},{3,4},{4,5},{5,6},{6,7},{7,8},{8,9},{9,10... | collective-permute-start | bytes 2359304 | tf_op jit(solution)/shard_map/ppermute | solution.py:21
  47.9 7.0 %gather_fusion.1 = f32[2304,512]{1,0:T(8,128)} fusion(f32[64,512]{1,0:T(8,128)S(1)} %fusion.121, s32[3072]{0:T(1024)S(1)} %pad_clamp_fusion), kind=kCustom, calls=%fused_computation.1 | custom fusion | bytes 9446400 | tf_op jit(solution)/shard_map/jit(_take)/gather | solution.py:325
  55.0 2.1 collective-permute-done.3
  57.1 2.6 %collective-permute-done.2 = bf16[3,256,512]{2,1,0:T(8,128)(2,1)} collective-permute-done((bf16[3,256,512]{2,1,0:T(8,128)(2,1)S(1)}, bf16[3,256,512]{2,1,0:T(8,128)(2,1)}, u32[]{:S(2)}, u32[]{:S(2)}) %collective-permute-start.2) | collective-permute-done | bytes 786464 | tf_op jit(solution)/shard_map/ppermute | solution.py:21
  59.6 1.8 pad_maximum_fusion.1
  62.4 3.9 %fusion.5 = (bf16[2304,512]{1,0:T(8,128)(2,1)S(1)}, f32[2304,512]{1,0:T(8,128)}) fusion(bf16[4,512]{1,0:T(4,128)(2,1)S(1)} %copy-done.74, bf16[1,4,2304]{2,1,0:T(4,128)(2,1)S(1)} %copy-done.73, f32[2304,512]{1,0:T(8,128)S(1)} %copy-done.3, pred[2304]{0:T(1024)(128)(4,1)S(1)} %get-tuple-element.52, bf16[2304,512]{1,0:T(8,128)(2,1)S(1)} %bitcast.119), kind=kOutput, calls=%fused_computation.22 | convolution fusion | flops 20054016 | bytes 14180608 | tf_op jit(solution)/shard_map/dot_general | solution.py:25
  66.3 1.5 fusion.113
  68.4 1.6 copy-done.1
  70.0 1.4 fusion.20
  73.6 2.7 %collective-permute-start.4 = (bf16[16,512]{1,0:T(8,128)(2,1)S(1)}, bf16[16,512]{1,0:T(8,128)(2,1)S(1)}, u32[]{:S(2)}, u32[]{:S(2)}) collective-permute-start(bf16[16,512]{1,0:T(8,128)(2,1)S(1)} %get-tuple-element.50), channel_id=1, source_target_pairs={{0,32},{32,64},{64,96},{1,33},{33,65},{65,97},{2,34},{34,66},{66,9... | collective-permute-start | bytes 49160 | tf_op jit(solution)/shard_map/ppermute | solution.py:15
  76.4 1.3 collective-permute-start.5
  78.0 2.4 collective-permute-start.7
  80.4 1.6 gather_fusion.4
  82.2 2.0 gather_fusion.3
  89.7 2.5 fusion.24
  92.2 1.5 fusion.107
  96.5 4.7 %collective-permute-start.10 = (bf16[16,512]{1,0:T(8,128)(2,1)S(1)}, bf16[16,512]{1,0:T(8,128)(2,1)S(1)}, u32[]{:S(2)}, u32[]{:S(2)}) collective-permute-start(bf16[16,512]{1,0:T(8,128)(2,1)S(1)} %get-tuple-element.45), channel_id=1, source_target_pairs={{1,0},{2,1},{3,2},{4,3},{5,4},{6,5},{7,6},{8,7},{9,8},{10,9},{11,1... | collective-permute-start | bytes 49160 | tf_op jit(solution)/shard_map/ppermute | solution.py:21
  101.2 4.3 %collective-permute-start.9 = (bf16[16,512]{1,0:T(8,128)(2,1)S(1)}, bf16[16,512]{1,0:T(8,128)(2,1)S(1)}, u32[]{:S(2)}, u32[]{:S(2)}) collective-permute-start(bf16[16,512]{1,0:T(8,128)(2,1)S(1)} %get-tuple-element.46), channel_id=1, source_target_pairs={{0,32},{32,64},{64,96},{1,33},{33,65},{65,97},{2,34},{34,66},{66,9... | collective-permute-start | bytes 49160 | tf_op jit(solution)/shard_map/ppermute | solution.py:15
  105.5 1.5 collective-permute-start.8
  107.4 2.6 %collective-permute-done.8 = bf16[16,512]{1,0:T(8,128)(2,1)S(1)} collective-permute-done((bf16[16,512]{1,0:T(8,128)(2,1)S(1)}, bf16[16,512]{1,0:T(8,128)(2,1)S(1)}, u32[]{:S(2)}, u32[]{:S(2)}) %collective-permute-start.8) | collective-permute-done | bytes 16416 | tf_op jit(solution)/shard_map/ppermute | solution.py:15
  111.4 6.3 %fusion.106 = (f32[2304]{0:T(1024)S(1)}, f32[2304]{0:T(1024)S(1)}, f32[2304,512]{0,1:T(8,128)}) fusion(f32[2304]{0:T(1024)} %copy-done.38, f32[2304,512]{0,1:T(8,128)} %copy-done.1, f32[2304]{0:T(1024)S(1)} %broadcast_multiply_fusion.2, f32[512]{0:T(512)S(1)} %copy-done.63, bf16[64,512]{1,0:T(8,128)(2,1)S(1)} %fusion.18, ...), kind=kOutput, calls=%fused_computation.200 | convolution fusion | flops 191770112 | bytes 10078208 | tf_op jit(solution)/shard_map/dot_general | solution.py:396
  117.7 4.8 %multiply_convert_fusion = bf16[2304,512]{0,1:T(8,128)(2,1)S(1)} fusion(f32[2304,512]{0,1:T(8,128)} %get-tuple-element.72, f32[2304,512]{0,1:T(8,128)} %copy-done.1, f32[2304]{0:T(1024)S(1)} %broadcast_multiply_fusion, f32[2304]{0:T(1024)S(1)} %broadcast_multiply_fusion.1, f32[2304]{0:T(1024)S(1)} %copy-done.39, f32[2304]{0:T(1024)S(1)} %broadcast_multiply_fusion.2), kind=kLoop, calls=%fused_computation.12 | loop fusion | flops 8257536 | bytes 11833344 | tf_op jit(solution)/shard_map/convert_element_type | solution.py:58
  122.6 6.0 %convolution_multiply_fusion = bf16[2304,512]{1,0:T(8,128)(2,1)S(1)} fusion(bf16[2304,512]{0,1:T(8,128)(2,1)S(1)} %multiply_convert_fusion, bf16[512,512]{1,0:T(8,128)(2,1)S(1)} %copy-done.30, f32[2304,512]{1,0:T(8,128)} %get-tuple-element.57), kind=kOutput, calls=%fused_computation.6 | convolution fusion | flops 1218576384 | bytes 9961472 | tf_op jit(solution)/shard_map/dot_general | solution.py:35
  128.6 1.4 slice_bitcast_fusion.5
  130.1 6.4 %collective-permute-start.13 = (bf16[3,256,512]{2,1,0:T(8,128)(2,1)}, bf16[3,256,512]{2,1,0:T(8,128)(2,1)}, u32[]{:S(2)}, u32[]{:S(2)}) collective-permute-start(bf16[3,256,512]{2,1,0:T(8,128)(2,1)} %get-tuple-element.34), channel_id=1, source_target_pairs={{1,0},{2,1},{3,2},{4,3},{5,4},{6,5},{7,6},{8,7},{9,8},{10,9},{11,1... | collective-permute-start | bytes 2359304 | tf_op jit(solution)/shard_map/ppermute | solution.py:21
  136.5 2.2 fusion.125.refs_4_
  138.7 2.7 %fusion.126.refs_5_ = f32[512,512]{1,0:T(8,128)} fusion(bf16[512,512]{1,0:T(8,128)(2,1)} %copy-done.4, bf16[512,512]{0,1:T(8,128)(2,1)} %copy-done.17), kind=kOutput, calls=%fused_computation.218 | convolution fusion | flops 268435456 | bytes 2097152 | tf_op jit(solution)/shard_map/dot_general | solution.py:25
  141.8 3.9 %collective-permute-done.12 = bf16[3,256,512]{2,1,0:T(8,128)(2,1)} collective-permute-done((bf16[3,256,512]{2,1,0:T(8,128)(2,1)}, bf16[3,256,512]{2,1,0:T(8,128)(2,1)}, u32[]{:S(2)}, u32[]{:S(2)}) %collective-permute-start.12) | collective-permute-done | bytes 786464 | tf_op jit(solution)/shard_map/ppermute | solution.py:21
  145.8 1.6 pad_maximum_fusion.2
  147.4 1.5 slice_bitcast_fusion.2
  150.2 4.9 %collective-permute-start.14 = (bf16[3,256,512]{2,1,0:T(8,128)(2,1)}, bf16[3,256,512]{2,1,0:T(8,128)(2,1)}, u32[]{:S(2)}, u32[]{:S(2)}) collective-permute-start(bf16[3,256,512]{2,1,0:T(8,128)(2,1)} %get-tuple-element.30), channel_id=1, source_target_pairs={{0,32},{32,64},{64,96},{1,33},{33,65},{65,97},{2,34},{34,66},{66,9... | collective-permute-start | bytes 2359304 | tf_op jit(solution)/shard_map/ppermute | solution.py:15
  155.1 1.3 fusion.124.refs_3_
  156.3 2.0 convolution_bitcast_fusion.refs_1_
  158.4 4.9 %fusion.123.refs_2_ = f32[512,512]{1,0:T(8,128)} fusion(bf16[2304,512]{1,0:T(8,128)(2,1)} %copy-done.2, bf16[2304,512]{0,1:T(8,128)(2,1)} %copy-done.12), kind=kOutput, calls=%fused_computation.215 | convolution fusion | flops 1207959552 | bytes 5767168 | tf_op jit(solution)/shard_map/dot_general | solution.py:25
  165.3 3.0 %pad_maximum_fusion.3 = bf16[3,3,256,512]{3,2,1,0:T(8,128)(2,1)} fusion(bf16[1,3,256,512]{3,2,1,0:T(8,128)(2,1)} %bitcast.34, bf16[1,3,256,512]{3,2,1,0:T(8,128)(2,1)S(1)} %copy-done.8, bf16[1,3,256,512]{3,2,1,0:T(8,128)(2,1)} %bitcast.32), kind=kLoop, calls=%fused_computation.26 | loop fusion | flops 2359296 | bytes 4718592 | tf_op jit(solution)/shard_map/stack | solution.py:93
  168.3 21.1 %scatter_custom_fusion = f32[1024,512]{1,0:T(8,128)S(1)} fusion(s32[2304]{0:T(1024)} %copy-done.43, bf16[2304,512]{1,0:T(8,128)(2,1)} %bitcast.116, f32[]{:T(128)} %constant.97.clone.1, pred[2304]{0:T(1024)(128)(4,1)S(1)} %ge.68), kind=kCustom, calls=%fused_computation.10 | custom fusion | flops 3538944 | bytes 4459776 | tf_op jit(solution)/shard_map/scatter-add | solution.py:407
  189.4 3.1 %fusion.35 = f32[1024,512]{1,0:T(8,128)} fusion(bf16[512,512]{1,0:T(8,128)(2,1)} %param.33, f32[1024,512]{1,0:T(8,128)S(1)} %scatter_custom_fusion), kind=kOutput, calls=%fused_computation.80 | convolution fusion | flops 537395200 | bytes 4718592 | tf_op jit(solution)/shard_map/dot_general | solution.py:35
  192.6 1.7 convolution_bitcast_fusion.1.refs_0_
  194.3 48.5 %reduce.9.full = bf16[6,2,4,4,4,16,128]{6,5,4,3,2,1,0:T(8,128)(2,1)} custom-call(f32[512,512]{1,0:T(8,128)} %convolution_bitcast_fusion.1.refs_0_, f32[512,512]{1,0:T(8,128)} %convolution_bitcast_fusion.refs_1_, f32[512,512]{1,0:T(8,128)} %fusion.123.refs_2_, f32[512,512]{1,0:T(8,128)} %fusion.124.refs_3_, f32[512,512]{1,0:T(8,128)} %fusion.125.refs_4_, ...), custom_call_target="tpu_custom_call" | custom-call | tf_op jit(solution)/shard_map/reduce/pallas_call | solution.py:263
  242.7 7.7 %spread.1 = (f32[512,512]{1,0:T(8,128)}, f32[512,512]{1,0:T(8,128)}, f32[512,512]{1,0:T(8,128)}, f32[512,512]{1,0:T(8,128)}, f32[512,512]{1,0:T(8,128)}, /*index=5*/f32[512,512]{1,0:T(8,128)}) custom-call(bf16[6,2,4,4,4,16,128]{6,5,4,3,2,1,0:T(8,128)(2,1)} %reduce.9.full), custom_call_target="tpu_custom_call" | custom-call | tf_op jit(solution)/shard_map/spread/pallas_call | solution.py:272
  (235 shorter events, 22.7 us)
Async XLA Ops:
  15.6 7.7 %copy-start.51 = (s32[1,9,256]{2,0,1:T(1,128)S(1)}, s32[1,9,256]{2,0,1:T(1,128)}, u32[]{:S(2)}) copy-start(s32[1,9,256]{2,0,1:T(1,128)} %param.27) | copy-start | bytes 27652
  15.6 7.8 %copy-start.52 = (s32[1,4,16]{2,1,0:T(4,128)S(1)}, s32[1,4,16]{2,1,0:T(4,128)}, u32[]{:S(2)}) copy-start(s32[1,4,16]{2,1,0:T(4,128)} %param.29) | copy-start | bytes 772
  15.6 7.9 %copy-start.40 = (s32[1,512]{1,0:T(1,128)S(1)}, s32[1,512]{1,0:T(1,128)}, u32[]{:S(2)}) copy-start(s32[1,512]{1,0:T(1,128)} %param.31) | copy-start | bytes 6148
  15.6 7.9 %copy-start.48 = (s32[1,512]{1,0:T(1,128)S(1)}, s32[1,512]{1,0:T(1,128)}, u32[]{:S(2)}) copy-start(s32[1,512]{1,0:T(1,128)} %param.30) | copy-start | bytes 6148
  15.6 7.9 %copy-start.20 = (bf16[64,512]{1,0:T(8,128)(2,1)S(1)}, bf16[64,512]{1,0:T(8,128)(2,1)}, u32[]{:S(2)}) copy-start(bf16[64,512]{1,0:T(8,128)(2,1)} %param.25) | copy-start | bytes 196612
  15.7 7.9 %copy-start.32 = (bf16[512,512]{1,0:T(8,128)(2,1)S(1)}, bf16[512,512]{1,0:T(8,128)(2,1)}, u32[]{:S(2)}) copy-start(bf16[512,512]{1,0:T(8,128)(2,1)} %param.34) | copy-start | bytes 1572868
  16.8 20.9 %collective-permute-start.1 = (bf16[3,256,512]{2,1,0:T(8,128)(2,1)}, bf16[3,256,512]{2,1,0:T(8,128)(2,1)}, u32[]{:S(2)}, u32[]{:S(2)}) collective-permute-start(bf16[3,256,512]{2,1,0:T(8,128)(2,1)} %get-tuple-element.40), channel_id=1, source_target_pairs={{0,32},{32,64},{64,96},{1,33},{33,65},{65,97},{2,34},{34,66},{66,9... | collective-permute-start | bytes 2359304 | tf_op jit(solution)/shard_map/ppermute | solution.py:15
  22.0 20.1 %collective-permute-start = (bf16[3,256,512]{2,1,0:T(8,128)(2,1)S(1)}, bf16[3,256,512]{2,1,0:T(8,128)(2,1)}, u32[]{:S(2)}, u32[]{:S(2)}) collective-permute-start(bf16[3,256,512]{2,1,0:T(8,128)(2,1)S(1)} %get-tuple-element.39), channel_id=1, source_target_pairs={{32,0},{64,32},{96,64},{33,1},{65,33},{97,65},{34,2},{66,34},{98,6... | collective-permute-start | bytes 2359304 | tf_op jit(solution)/shard_map/ppermute | solution.py:15
  44.8 12.2 %collective-permute-start.3 = (bf16[3,256,512]{2,1,0:T(8,128)(2,1)}, bf16[3,256,512]{2,1,0:T(8,128)(2,1)}, u32[]{:S(2)}, u32[]{:S(2)}) collective-permute-start(bf16[3,256,512]{2,1,0:T(8,128)(2,1)} %get-tuple-element.37), channel_id=1, source_target_pairs={{31,0},{0,1},{1,2},{2,3},{3,4},{4,5},{5,6},{6,7},{7,8},{8,9},{9,10... | collective-permute-start | bytes 2359304 | tf_op jit(solution)/shard_map/ppermute | solution.py:21
  47.8 11.8 %collective-permute-start.2 = (bf16[3,256,512]{2,1,0:T(8,128)(2,1)S(1)}, bf16[3,256,512]{2,1,0:T(8,128)(2,1)}, u32[]{:S(2)}, u32[]{:S(2)}) collective-permute-start(bf16[3,256,512]{2,1,0:T(8,128)(2,1)S(1)} %get-tuple-element.36), channel_id=1, source_target_pairs={{1,0},{2,1},{3,2},{4,3},{5,4},{6,5},{7,6},{8,7},{9,8},{10,9},{11,1... | collective-permute-start | bytes 2359304 | tf_op jit(solution)/shard_map/ppermute | solution.py:21
  47.9 7.0 %copy-start.64 = (s32[64]{0:T(128)}, s32[64]{0:T(128)S(1)}, u32[]{:S(2)}) copy-start(s32[64]{0:T(128)S(1)} %reshape_squeeze.6) | copy-start | bytes 772
  47.9 20.5 %copy-start.34 = (s32[2304]{0:T(1024)}, s32[2304]{0:T(1024)S(1)}, u32[]{:S(2)}) copy-start(s32[2304]{0:T(1024)S(1)} %eq.56) | copy-start | bytes 27652
  47.9 13.5 %copy-start.73 = (bf16[1,4,2304]{2,1,0:T(4,128)(2,1)S(1)}, bf16[1,4,2304]{2,1,0:T(4,128)(2,1)}, u32[]{:S(2)}) copy-start(bf16[1,4,2304]{2,1,0:T(4,128)(2,1)} %param.28) | copy-start | bytes 55300
  47.9 13.5 %copy-start.74 = (bf16[4,512]{1,0:T(4,128)(2,1)S(1)}, bf16[4,512]{1,0:T(4,128)(2,1)}, u32[]{:S(2)}) copy-start(bf16[4,512]{1,0:T(4,128)(2,1)} %param.35) | copy-start | bytes 12292
  54.9 29.2 %copy-start.66 = (pred[512]{0:T(512)(128)(4,1)}, pred[512]{0:T(512)(128)(4,1)S(1)}, u32[]{:S(2)}) copy-start(pred[512]{0:T(512)(128)(4,1)S(1)} %get-tuple-element.77) | copy-start | bytes 1540
  55.0 29.2 %copy-start.68 = (pred[512]{0:T(512)(128)(4,1)}, pred[512]{0:T(512)(128)(4,1)S(1)}, u32[]{:S(2)}) copy-start(pred[512]{0:T(512)(128)(4,1)S(1)} %get-tuple-element.78) | copy-start | bytes 1540
  72.1 9.9 %copy-start.53 = (f32[64]{0:T(128)}, f32[64]{0:T(128)S(1)}, u32[]{:S(2)}) copy-start(f32[64]{0:T(128)S(1)} %broadcast_multiply_fusion.11) | copy-start | bytes 772
  72.4 9.7 %copy-start.58 = (f32[64]{0:T(128)}, f32[64]{0:T(128)S(1)}, u32[]{:S(2)}) copy-start(f32[64]{0:T(128)S(1)} %add_rsqrt_fusion.3) | copy-start | bytes 772
  73.6 8.5 %collective-permute-start.4 = (bf16[16,512]{1,0:T(8,128)(2,1)S(1)}, bf16[16,512]{1,0:T(8,128)(2,1)S(1)}, u32[]{:S(2)}, u32[]{:S(2)}) collective-permute-start(bf16[16,512]{1,0:T(8,128)(2,1)S(1)} %get-tuple-element.50), channel_id=1, source_target_pairs={{0,32},{32,64},{64,96},{1,33},{33,65},{65,97},{2,34},{34,66},{66,9... | collective-permute-start | bytes 49160 | tf_op jit(solution)/shard_map/ppermute | solution.py:15
  76.4 5.6 %collective-permute-start.5 = (bf16[16,512]{1,0:T(8,128)(2,1)S(1)}, bf16[16,512]{1,0:T(8,128)(2,1)S(1)}, u32[]{:S(2)}, u32[]{:S(2)}) collective-permute-start(bf16[16,512]{1,0:T(8,128)(2,1)S(1)} %get-tuple-element.49), channel_id=1, source_target_pairs={{32,0},{64,32},{96,64},{33,1},{65,33},{97,65},{34,2},{66,34},{98,6... | collective-permute-start | bytes 49160 | tf_op jit(solution)/shard_map/ppermute | solution.py:15
  77.7 4.4 %collective-permute-start.6 = (bf16[16,512]{1,0:T(8,128)(2,1)S(1)}, bf16[16,512]{1,0:T(8,128)(2,1)S(1)}, u32[]{:S(2)}, u32[]{:S(2)}) collective-permute-start(bf16[16,512]{1,0:T(8,128)(2,1)S(1)} %get-tuple-element.48), channel_id=1, source_target_pairs={{31,0},{0,1},{1,2},{2,3},{3,4},{4,5},{5,6},{6,7},{7,8},{8,9},{9,10... | collective-permute-start | bytes 49160 | tf_op jit(solution)/shard_map/ppermute | solution.py:21
  78.0 4.1 %collective-permute-start.7 = (bf16[16,512]{1,0:T(8,128)(2,1)S(1)}, bf16[16,512]{1,0:T(8,128)(2,1)S(1)}, u32[]{:S(2)}, u32[]{:S(2)}) collective-permute-start(bf16[16,512]{1,0:T(8,128)(2,1)S(1)} %get-tuple-element.47), channel_id=1, source_target_pairs={{1,0},{2,1},{3,2},{4,3},{5,4},{6,5},{7,6},{8,7},{9,8},{10,9},{11,1... | collective-permute-start | bytes 49160 | tf_op jit(solution)/shard_map/ppermute | solution.py:21
  94.9 12.1 %copy-start.42 = (s32[1,512]{1,0:T(1,128)S(1)}, s32[1,512]{1,0:T(1,128)}, u32[]{:S(2)}) copy-start(s32[1,512]{1,0:T(1,128)} %param.31) | copy-start | bytes 6148
  94.9 15.1 %copy-start.65 = (s32[64]{0:T(128)S(1)}, s32[64]{0:T(128)}, u32[]{:S(2)}) copy-start(s32[64]{0:T(128)} %copy-done.64) | copy-start | bytes 772
  94.9 15.4 %copy-start.14 = (bf16[512,512]{1,0:T(8,128)(2,1)S(1)}, bf16[512,512]{1,0:T(8,128)(2,1)}, u32[]{:S(2)}) copy-start(bf16[512,512]{1,0:T(8,128)(2,1)} %param.41) | copy-start | bytes 1572868
  94.9 15.4 %copy-start.21 = (f32[64,1024]{1,0:T(8,128)S(1)}, f32[64,1024]{1,0:T(8,128)}, u32[]{:S(2)}) copy-start(f32[64,1024]{1,0:T(8,128)} %fusion.24) | copy-start | bytes 786436
  94.9 15.4 %copy-start.25 = (bf16[64,512]{1,0:T(8,128)(2,1)S(1)}, bf16[64,512]{1,0:T(8,128)(2,1)}, u32[]{:S(2)}) copy-start(bf16[64,512]{1,0:T(8,128)(2,1)} %param.32) | copy-start | bytes 196612
  95.8 14.8 %copy-start.16 = (bf16[512,512]{1,0:T(8,128)(2,1)S(1)}, bf16[512,512]{1,0:T(8,128)(2,1)}, u32[]{:S(2)}) copy-start(bf16[512,512]{1,0:T(8,128)(2,1)} %param.42) | copy-start | bytes 1572868
  95.8 14.8 %copy-start.47 = (f32[512]{0:T(512)S(1)}, f32[512]{0:T(512)}, u32[]{:S(2)}) copy-start(f32[512]{0:T(512)} %param.40) | copy-start | bytes 6148
  95.8 14.8 %copy-start.55 = (f32[64]{0:T(128)S(1)}, f32[64]{0:T(128)}, u32[]{:S(2)}) copy-start(f32[64]{0:T(128)} %copy-done.53) | copy-start | bytes 772
  95.8 14.8 %copy-start.60 = (f32[64]{0:T(128)S(1)}, f32[64]{0:T(128)}, u32[]{:S(2)}) copy-start(f32[64]{0:T(128)} %copy-done.58) | copy-start | bytes 772
  95.8 15.2 %copy-start.37 = (f32[64,512]{1,0:T(8,128)S(1)}, f32[64,512]{1,0:T(8,128)}, u32[]{:S(2)}) copy-start(f32[64,512]{1,0:T(8,128)} %copy-done.36) | copy-start | bytes 393220
  95.9 15.2 %copy-start.72 = (bf16[512,512]{1,0:T(8,128)(2,1)S(1)}, bf16[512,512]{1,0:T(8,128)(2,1)}, u32[]{:S(2)}) copy-start(bf16[512,512]{1,0:T(8,128)(2,1)} %param.39) | copy-start | bytes 1572868
  96.2 15.1 %copy-start.11 = (bf16[1024,512]{1,0:T(8,128)(2,1)S(1)}, bf16[1024,512]{1,0:T(8,128)(2,1)}, u32[]{:S(2)}) copy-start(bf16[1024,512]{1,0:T(8,128)(2,1)} %param.38) | copy-start | bytes 3145732
  96.2 15.1 %copy-start.63 = (f32[512]{0:T(512)S(1)}, f32[512]{0:T(512)}, u32[]{:S(2)}) copy-start(f32[512]{0:T(512)} %param.37) | copy-start | bytes 6148
  96.3 11.1 %collective-permute-start.11 = (bf16[16,512]{1,0:T(8,128)(2,1)S(1)}, bf16[16,512]{1,0:T(8,128)(2,1)S(1)}, u32[]{:S(2)}, u32[]{:S(2)}) collective-permute-start(bf16[16,512]{1,0:T(8,128)(2,1)S(1)} %get-tuple-element.44), channel_id=1, source_target_pairs={{31,0},{0,1},{1,2},{2,3},{3,4},{4,5},{5,6},{6,7},{7,8},{8,9},{9,10... | collective-permute-start | bytes 49160 | tf_op jit(solution)/shard_map/ppermute | solution.py:21
  96.5 10.9 %collective-permute-start.10 = (bf16[16,512]{1,0:T(8,128)(2,1)S(1)}, bf16[16,512]{1,0:T(8,128)(2,1)S(1)}, u32[]{:S(2)}, u32[]{:S(2)}) collective-permute-start(bf16[16,512]{1,0:T(8,128)(2,1)S(1)} %get-tuple-element.45), channel_id=1, source_target_pairs={{1,0},{2,1},{3,2},{4,3},{5,4},{6,5},{7,6},{8,7},{9,8},{10,9},{11,1... | collective-permute-start | bytes 49160 | tf_op jit(solution)/shard_map/ppermute | solution.py:21
  101.2 6.2 %collective-permute-start.9 = (bf16[16,512]{1,0:T(8,128)(2,1)S(1)}, bf16[16,512]{1,0:T(8,128)(2,1)S(1)}, u32[]{:S(2)}, u32[]{:S(2)}) collective-permute-start(bf16[16,512]{1,0:T(8,128)(2,1)S(1)} %get-tuple-element.46), channel_id=1, source_target_pairs={{0,32},{32,64},{64,96},{1,33},{33,65},{65,97},{2,34},{34,66},{66,9... | collective-permute-start | bytes 49160 | tf_op jit(solution)/shard_map/ppermute | solution.py:15
  105.5 4.5 %collective-permute-start.8 = (bf16[16,512]{1,0:T(8,128)(2,1)S(1)}, bf16[16,512]{1,0:T(8,128)(2,1)S(1)}, u32[]{:S(2)}, u32[]{:S(2)}) collective-permute-start(bf16[16,512]{1,0:T(8,128)(2,1)S(1)} %get-tuple-element.43), channel_id=1, source_target_pairs={{32,0},{64,32},{96,64},{33,1},{65,33},{97,65},{34,2},{66,34},{98,6... | collective-permute-start | bytes 49160 | tf_op jit(solution)/shard_map/ppermute | solution.py:15
  110.3 7.4 %copy-start.22 = (bf16[64,512]{1,0:T(8,128)(2,1)}, bf16[64,512]{1,0:T(8,128)(2,1)S(1)}, u32[]{:S(2)}) copy-start(bf16[64,512]{1,0:T(8,128)(2,1)S(1)} %fusion.23) | copy-start | bytes 196612
  128.6 7.9 %copy-start.50 = (pred[9,256]{1,0:T(8,128)(4,1)S(1)}, pred[9,256]{1,0:T(8,128)(4,1)}, u32[]{:S(2)}) copy-start(pred[9,256]{1,0:T(8,128)(4,1)} %get-tuple-element.53) | copy-start | bytes 6916
  130.1 11.7 %collective-permute-start.13 = (bf16[3,256,512]{2,1,0:T(8,128)(2,1)}, bf16[3,256,512]{2,1,0:T(8,128)(2,1)}, u32[]{:S(2)}, u32[]{:S(2)}) collective-permute-start(bf16[3,256,512]{2,1,0:T(8,128)(2,1)} %get-tuple-element.34), channel_id=1, source_target_pairs={{1,0},{2,1},{3,2},{4,3},{5,4},{6,5},{7,6},{8,7},{9,8},{10,9},{11,1... | collective-permute-start | bytes 2359304 | tf_op jit(solution)/shard_map/ppermute | solution.py:21
  136.5 9.3 %collective-permute-start.12 = (bf16[3,256,512]{2,1,0:T(8,128)(2,1)}, bf16[3,256,512]{2,1,0:T(8,128)(2,1)}, u32[]{:S(2)}, u32[]{:S(2)}) collective-permute-start(bf16[3,256,512]{2,1,0:T(8,128)(2,1)} %get-tuple-element.33), channel_id=1, source_target_pairs={{31,0},{0,1},{1,2},{2,3},{3,4},{4,5},{5,6},{6,7},{7,8},{8,9},{9,10... | collective-permute-start | bytes 2359304 | tf_op jit(solution)/shard_map/ppermute | solution.py:21
  136.5 9.2 %copy-start.9 = (bf16[3,1,256,512]{3,2,0,1:T(8,128)(2,1)S(1)}, bf16[3,1,256,512]{3,2,0,1:T(8,128)(2,1)}, u32[]{:S(2)}) copy-start(bf16[3,1,256,512]{3,2,0,1:T(8,128)(2,1)} %get-tuple-element.35) | copy-start | bytes 2359300
  147.4 7.7 %copy-start.23 = (bf16[64,512]{1,0:T(8,128)(2,1)S(1)}, bf16[64,512]{1,0:T(8,128)(2,1)}, u32[]{:S(2)}) copy-start(bf16[64,512]{1,0:T(8,128)(2,1)} %copy-done.22) | copy-start | bytes 196612
  147.4 9.0 %copy-start.35 = (s32[2304]{0:T(1024)S(1)}, s32[2304]{0:T(1024)}, u32[]{:S(2)}) copy-start(s32[2304]{0:T(1024)} %copy-done.34) | copy-start | bytes 27652
  148.9 15.5 %collective-permute-start.15 = (bf16[3,256,512]{2,1,0:T(8,128)(2,1)}, bf16[3,256,512]{2,1,0:T(8,128)(2,1)}, u32[]{:S(2)}, u32[]{:S(2)}) collective-permute-start(bf16[3,256,512]{2,1,0:T(8,128)(2,1)} %get-tuple-element.31), channel_id=1, source_target_pairs={{32,0},{64,32},{96,64},{33,1},{65,33},{97,65},{34,2},{66,34},{98,6... | collective-permute-start | bytes 2359304 | tf_op jit(solution)/shard_map/ppermute | solution.py:15
  150.2 15.1 %collective-permute-start.14 = (bf16[3,256,512]{2,1,0:T(8,128)(2,1)}, bf16[3,256,512]{2,1,0:T(8,128)(2,1)}, u32[]{:S(2)}, u32[]{:S(2)}) collective-permute-start(bf16[3,256,512]{2,1,0:T(8,128)(2,1)} %get-tuple-element.30), channel_id=1, source_target_pairs={{0,32},{32,64},{64,96},{1,33},{33,65},{65,97},{2,34},{34,66},{66,9... | collective-permute-start | bytes 2359304 | tf_op jit(solution)/shard_map/ppermute | solution.py:15
  (43 other events, 97.4 us)

commit v2 on v0

v2 whole, which is shorter than its diff:
```python
import functools

import jax
import jax.numpy as jnp
from jax import lax
from jax.experimental import pallas as pl
from jax.experimental.pallas import tpu as pltpu
from jax.sharding import PartitionSpec as P

EPSILON = 1e-05
MESH = pl.DeviceIdType.MESH
ORDERS = ((0, 1, 2), (1, 2, 0), (2, 0, 1))
BF = jnp.bfloat16
F32 = jnp.float32


def mm(a, b):
    return jnp.dot(a, b, preferred_element_type=F32)


def mm_t(a, b):
    return lax.dot_general(a, b, (((0,), (0,)), ((), ())), preferred_element_type=F32)


def mm_nt(a, b):
    return lax.dot_general(a, b, (((1,), (1,)), ((), ())), preferred_element_type=F32)


def tail_forward(pre, weight):
    sig = jax.nn.sigmoid(pre)
    hid = (pre * sig).astype(BF)
    z = mm(hid, weight)
    centre = z - jnp.mean(z, axis=-1, keepdims=True)
    inv = lax.rsqrt(jnp.mean(centre * centre, axis=-1, keepdims=True) + EPSILON)
    return hid, centre * inv, inv, sig + pre * sig * (1.0 - sig)


def tail_backward(grad, gain, zhat, inv, slope, weight):
    u = grad * gain
    m1 = jnp.mean(u, axis=-1, keepdims=True)
    m2 = jnp.mean(u * zhat, axis=-1, keepdims=True)
    dz = (inv * (u - m1 - zhat * m2)).astype(BF)
    return dz, mm_nt(dz, weight) * slope


def coordinates():
    lon = lax.axis_index("lon")
    return (lax.axis_index("lat"), lon // 8, lax.rem(lon // 2, 4), lax.rem(lon, 2))


def device(z, x, y, c):
    return (z, (x * 4 + y) * 2 + c)


def ring_peer(me, dim, step):
    spot = list(me)
    spot[dim] = lax.rem(me[dim] + step, 4)
    return device(*spot)


def core_peer(me):
    return device(me[0], me[1], me[2], 1 - me[3])


def tile_peer(dlat, dlon):
    return (lax.rem(lax.axis_index("lat") + dlat + 4, 4), lax.rem(lax.axis_index("lon") + dlon + 32, 32))


def offset_peer(k, sign):
    return tile_peer(sign * (k // 3 - 1), sign * (lax.rem(k, 3) - 1))


def greet(peers):
    barrier = pltpu.get_barrier_semaphore()
    for peer in peers:
        pl.semaphore_signal(barrier, inc=1, device_id=peer, device_id_type=MESH)
    pl.semaphore_wait(barrier, len(peers))


def push(src, dst, send, recv, peer):
    return pltpu.make_async_remote_copy(
        src_ref=src, dst_ref=dst, send_sem=send, recv_sem=recv, device_id=peer, device_id_type=MESH
    )


class Reduction:
    def __init__(self, order, source, bufs, send, recv):
        self.order, self.source = ORDERS[order], source
        self.s0, self.r0, self.s1, self.r1, self.s2, self.r2, self.s3, self.r3, self.full = bufs
        self.send, self.recv = send, recv

    def copy(self, slot):
        me = coordinates()
        spot = [me[d] for d in self.order]
        if slot == 0:
            src, dst, peer = self.s0, self.r0, core_peer(me)
        elif slot < 10:
            level, step = (slot - 1) // 3, (slot - 1) % 3 + 1
            sends = (self.s1, self.s2, self.s3)[level]
            lands = (self.r1, self.r2, self.r3)[level]
            src, dst = sends.at[lax.rem(spot[level] + step, 4)], lands.at[step - 1]
            peer = ring_peer(me, self.order[level], step)
        else:
            level = 3 - (slot - 10) // 3
            src = dst = self.full.at[(me[3], *spot)[: level + 1]]
            step = (slot - 10) % 3 + 1
            peer = core_peer(me) if level == 0 else ring_peer(me, self.order[level - 1], step)
        return push(src, dst, self.send.at[slot], self.recv.at[slot], peer)

    def arrive(self, base):
        for k in range(3):
            self.copy(base + k).wait_recv()

    def depart(self, base):
        for step in (1, 3, 2):
            self.copy(base + step - 1).start()

    def begin(self):
        other = pl.multiple_of((1 - coordinates()[3]) * 256, 256)
        self.s0[...] = self.source[pl.ds(other, 256), :].astype(BF)
        self.copy(0).start()

    def scatter(self, level):
        me = coordinates()
        spot = [me[d] for d in self.order]
        if level == 0:
            self.copy(0).wait_recv()
            mine = pl.multiple_of(me[3] * 256, 256)
            total = self.source[pl.ds(mine, 256), :] + self.r0[...].astype(F32)
            self.s1[...] = total.astype(BF).reshape(4, 64, 512)
        else:
            self.arrive(3 * level - 2)
            sends, lands = (self.s1, self.s2)[level - 1], (self.r1, self.r2)[level - 1]
            total = sends[spot[level - 1]].astype(F32)
            for k in range(3):
                total = total + lands[k].astype(F32)
            total = total.astype(BF)
            if level == 1:
                self.s2[...] = total.reshape(4, 16, 512)
            else:
                for j in range(4):
                    self.s3[j] = total[:, j * 128 : (j + 1) * 128]
        self.depart(3 * level + 1)

    def gather(self, level):
        if level == 3:
            me = coordinates()
            a, b, c = [me[d] for d in self.order]
            self.arrive(7)
            total = self.s3[c].astype(F32)
            for k in range(3):
                total = total + self.r3[k].astype(F32)
            self.full[me[3], a, b, c] = total.astype(BF)
        else:
            self.arrive(10 + 3 * (2 - level))
        if level == 0:
            self.copy(19).start()
        else:
            self.depart(10 + 3 * (3 - level))

    def finish(self):
        self.copy(19).wait_recv()
        for slot in range(20):
            self.copy(slot).wait_send()


def reduction_scratch(count):
    shapes = ((256, 512), (256, 512), (4, 64, 512), (3, 64, 512), (4, 16, 512), (3, 16, 512), (4, 16, 128), (3, 16, 128))
    return [pltpu.VMEM((count,) + s, BF) for s in shapes]


OWN = 4
INPUTS = 25


def ahead(i):
    return lax.rem(i + 5, 9)


def main_kernel(*refs):
    (grid_lat, mesh_lat, send_rows, aux, halo_row, from_row, to_row, cot, w_grid_send, w_grid_recv, w_feat, w_grid_out,
     gain_grid, w_node_in, w_node_out, gain_node, w_proc_send, w_proc_recv, w_proc_out, gain_proc, w_upd_in, w_upd_out,
     gain_upd) = refs[:23]
    full, d_terms, mesh_out = refs[23:26]
    red = refs[26:34]
    (red_send, red_recv, grads, mesh_in, aux_in, part_out, part_in, dsum_out, dsum_in, halo_out, table, back_out, back_in,
     terms, slots, recv_hl, hid_s, zhat_s, slope_s, inv_s, dpre_s, drecv_s, cols, ex_send, ex_recv) = refs[34:]
    me = coordinates()
    greet([offset_peer(k, 1) for k in range(9) if k != OWN] + [core_peer(me)] + [ring_peer(me, d, s) for d in range(3) for s in (1, 2, 3)])

    def mesh_copy(k):
        return push(mesh_lat, mesh_in.at[k], ex_send.at[0, k], ex_recv.at[0, k], offset_peer(k, -1))

    def aux_copy(k):
        return push(aux.at[k], aux_in.at[k], ex_send.at[1, k], ex_recv.at[1, k], offset_peer(k, -1))

    def part_copy(k):
        return push(part_out.at[k], part_in.at[k], ex_send.at[2, k], ex_recv.at[2, k], offset_peer(k, 1))

    def dsum_copy(k):
        return push(dsum_out, dsum_in.at[k], ex_send.at[3, k], ex_recv.at[3, k], offset_peer(k, -1))

    ways = ((1, 0), (-1, 0), (0, 1), (0, -1))

    def halo_copy(j):
        return push(halo_out.at[pl.ds(16 * j, 16)], table.at[pl.ds(64 + 16 * j, 16)], ex_send.at[4, j], ex_recv.at[4, j], tile_peer(*ways[j]))

    def back_copy(j):
        dlat, dlon = ways[j]
        return push(back_out.at[pl.ds(16 * j, 16)], back_in.at[pl.ds(16 * j, 16)], ex_send.at[5, j], ex_recv.at[5, j], tile_peer(-dlat, -dlon))

    def each(copy):
        for k in (0, 2, 6, 8, 1, 7, 3, 5):
            copy(k).start()

    each(aux_copy)
    each(mesh_copy)
    mesh_in[OWN] = mesh_lat[...]
    aux_in[OWN] = aux[OWN]

    def terms_body(i, carry):
        rows = pl.ds(pl.multiple_of(i * 256, 256), 256)
        terms[rows, :] = mm(grid_lat[rows, :], w_grid_send[...]).astype(BF)
        return carry

    lax.fori_loop(0, 4, terms_body, 0)
    padded = jnp.concatenate([send_rows[...].astype(F32), jnp.zeros((7, 256), F32)], axis=0)
    cols[...] = jnp.transpose(padded)

    def slots_body(k, carry):
        lane = lax.broadcasted_iota(jnp.int32, (256, 16), 1)
        col = jnp.sum(jnp.where(lane == k, cols[...], 0.0), axis=1, keepdims=True).astype(jnp.int32)
        pick = (col == lax.broadcasted_iota(jnp.int32, (256, 1024), 1)).astype(F32).astype(BF)
        slots[k] = mm(pick, terms[...]).astype(BF)
        return carry

    lax.fori_loop(0, 9, slots_body, 0)
    for k in range(9):
        if k != OWN:
            mesh_copy(k).wait_recv()
            aux_copy(k).wait_recv()

    def recv_body(k, carry):
        full_terms = mm(mesh_in[k], w_grid_recv[...])
        high = full_terms.astype(BF)
        recv_hl[k, :64, :] = high
        recv_hl[k, 64:, :] = (full_terms - high.astype(F32)).astype(BF)
        return carry

    lax.fori_loop(0, 9, recv_body, 0)

    def receivers(k):
        index = aux_in[k].astype(F32)[4:5, :].astype(jnp.int32)
        return (index == lax.broadcasted_iota(jnp.int32, (64, 256), 0)).astype(F32).astype(BF)

    def forward_body(i, carry):
        k = ahead(i)
        rec = receivers(k)
        left = jnp.concatenate([rec, rec, aux_in[k]], axis=0)
        right = jnp.concatenate([recv_hl[k], w_feat[...]], axis=0)
        pre = slots[k].astype(F32) + mm_t(left, right)
        hid, zhat, inv, slope = tail_forward(pre, w_grid_out[...])
        hid_s[k], zhat_s[k], slope_s[k] = hid, zhat.astype(BF), slope.astype(BF)
        inv_s[k] = inv
        part_out[k] = (mm(rec, zhat.astype(BF)) * gain_grid[...]).astype(BF)

        @pl.when(k != OWN)
        def _():
            part_copy(k).start()

        return carry

    lax.fori_loop(0, 9, forward_body, 0)

    grid_sum = part_out[OWN].astype(F32)
    for k in range(9):
        if k != OWN:
            part_copy(k).wait_recv()
            grid_sum = grid_sum + part_in[k].astype(F32)
    node_pre = mm(mesh_lat[...], w_node_in[:512, :]) + mm(grid_sum.astype(BF), w_node_in[512:, :])
    node_hid, node_zhat, node_inv, node_slope = tail_forward(node_pre, w_node_out[...])
    state = mesh_lat[...].astype(F32) + node_zhat * gain_node[...]
    state_bf = state.astype(BF)
    own_terms = mm(state_bf, w_proc_send[...]).astype(BF)
    lists = (halo_row[...] == lax.broadcasted_iota(jnp.int32, (64, 64), 0)).astype(F32).astype(BF)
    halo_out[...] = mm_t(lists, own_terms).astype(BF)
    for j in range(4):
        halo_copy(j).start()
    table[:64, :] = own_terms
    p_recv = mm(state_bf, w_proc_recv[...])
    p_high = p_recv.astype(BF)
    p_low = (p_recv - p_high.astype(F32)).astype(BF)
    pick_from = (from_row[...] == lax.broadcasted_iota(jnp.int32, (128, 512), 0)).astype(F32).astype(BF)
    pick_to = (to_row[...] == lax.broadcasted_iota(jnp.int32, (64, 512), 0)).astype(F32).astype(BF)
    for j in range(4):
        halo_copy(j).wait_recv()
    left = jnp.concatenate([pick_from, pick_to, pick_to], axis=0)
    right = jnp.concatenate([table[...], p_high, p_low], axis=0)
    proc_pre = mm_t(left, right)
    p_hid, p_zhat, p_inv, p_slope = tail_forward(proc_pre, w_proc_out[...])
    proc_sum = mm(pick_to, p_zhat.astype(BF)) * gain_proc[...]
    upd_pre = mm(state_bf, w_upd_in[:512, :]) + mm(proc_sum.astype(BF), w_upd_in[512:, :])
    upd_hid, upd_zhat, upd_inv, upd_slope = tail_forward(upd_pre, w_upd_out[...])
    mesh_out[...] = state + upd_zhat * gain_upd[...]
    top = cot[...].astype(F32)
    d_upd = tail_backward(top, gain_upd[...], upd_zhat, upd_inv, upd_slope, w_upd_out[...])[1].astype(BF)
    d_sum = mm_nt(d_upd, w_upd_in[512:, :])
    d_state = top + mm_nt(d_upd, w_upd_in[:512, :])
    d_msg = mm_t(pick_to, d_sum.astype(BF))
    dz, d_pre = tail_backward(d_msg, gain_proc[...], p_zhat, p_inv, p_slope, w_proc_out[...])
    d_pre = d_pre.astype(BF)
    d_table = mm(pick_from, d_pre)
    back_out[...] = d_table[64:, :].astype(BF)
    for j in range(4):
        back_copy(j).start()
    d_recv2 = mm(pick_to, d_pre).astype(BF)
    d_state = d_state + mm_nt(d_recv2, w_proc_recv[...])
    grads[3] = mm_t(p_hid, dz)
    grads[4] = mm_t(state_bf, d_recv2)
    for j in range(4):
        back_copy(j).wait_recv()
    d_own = (d_table[:64, :] + mm(lists, back_in[...])).astype(BF)
    d_state = d_state + mm_nt(d_own, w_proc_send[...])
    d_node = tail_backward(d_state, gain_node[...], node_zhat, node_inv, node_slope, w_node_out[...])[1].astype(BF)
    dsum_out[...] = mm_nt(d_node, w_node_in[512:, :]).astype(BF)
    each(dsum_copy)
    dsum_in[OWN] = dsum_out[...]
    grads[5] = mm_t(state_bf, d_own)
    parts = [
        Reduction(g % 3, grads.at[g], [b.at[g] for b in red] + [full.at[g]], red_send.at[g], red_recv.at[g])
        for g in range(6)
    ]
    early = parts[3:]
    for part in early:
        part.begin()

    grads[0] = jnp.zeros((512, 512), F32)
    grads[2] = jnp.zeros((512, 512), F32)
    stages = [functools.partial(Reduction.scatter, level=v) for v in range(3)] + [
        functools.partial(Reduction.gather, level=v) for v in (3, 2, 1, 0)
    ]

    def backward_body(i, carry):
        k = lax.rem(i + OWN, 9)

        @pl.when(k != OWN)
        def _():
            dsum_copy(k).wait_recv()

        for at, stage in enumerate(stages):

            @pl.when(i == at + 1)
            def _(stage=stage):
                for part in early:
                    stage(part)

        rec = receivers(k)
        grad = mm_t(rec, dsum_in[k])
        zhat = zhat_s[k].astype(F32)
        dz, dpre = tail_backward(grad, gain_grid[...], zhat, inv_s[k], slope_s[k].astype(F32), w_grid_out[...])
        grads[2] += mm_t(hid_s[k], dz)
        dpre = dpre.astype(BF)
        dpre_s[k] = dpre
        drecv_s[k] = mm(rec, dpre).astype(BF)
        return carry

    lax.fori_loop(0, 9, backward_body, 0)
    late = (parts[2], parts[1])
    parts[2].begin()
    grads[1] = mm_t(mesh_in[...].reshape(576, 512), drecv_s[...].reshape(576, 512))
    parts[1].begin()
    every = jnp.concatenate([send_rows[k : k + 1, :] for k in range(9)], axis=1)

    def terms_back(i, carry):
        rows = pl.ds(pl.multiple_of(i * 256, 256), 256)
        ids = lax.broadcasted_iota(jnp.int32, (256, 2304), 0) + i * 256
        put = (every == ids).astype(F32).astype(BF)
        d = mm(put, dpre_s[...].reshape(2304, 512)).astype(BF)
        d_terms[rows, :] = d
        grads[0] += mm_t(grid_lat[rows, :], d)
        return carry

    lax.fori_loop(0, 2, terms_back, 0)
    for part in late:
        stages[0](part)
    lax.fori_loop(2, 4, terms_back, 0)
    parts[0].begin()
    for at in range(1, 7):
        for part in late:
            stages[at](part)
        stages[at - 1](parts[0])
    stages[6](parts[0])
    for part in early:
        part.finish()
    for part in late:
        part.finish()
    parts[0].finish()
    for k in range(9):
        if k != OWN:
            for copy in (mesh_copy, aux_copy, part_copy, dsum_copy):
                copy(k).wait_send()
    for j in range(4):
        halo_copy(j).wait_send()
        back_copy(j).wait_send()


def finish_kernel(full, d_terms, w_grid_send, mesh_in, *outs):
    for g in range(6):
        for b in range(4):
            for c in range(4):
                outs[g][b * 16 : (b + 1) * 16, c * 128 : (c + 1) * 128] = full[g, 0, 0, b, c].astype(F32)
    outs[6][...] = mm_nt(d_terms[...], w_grid_send[...])
    outs[7][...] = mesh_in[...]


def local(
    grid_lat,
    mesh_lat,
    g2m_send,
    g2m_recv,
    g2m_feat,
    halo_lists,
    proc_send,
    proc_recv,
    cotangent,
    w_grid_send,
    w_grid_recv,
    w_grid_feat,
    w_grid_out,
    gain_grid,
    w_node_in,
    w_node_out,
    gain_node,
    w_proc_send,
    w_proc_recv,
    w_proc_out,
    gain_proc,
    w_upd_in,
    w_upd_out,
    gain_upd,
):
    feat = g2m_feat[0].reshape(4, 9, 256).transpose(1, 0, 2)
    recv = g2m_recv[0][:, None, :].astype(BF)
    aux = jnp.concatenate([feat, recv, jnp.zeros((9, 11, 256), BF)], axis=1)
    w_feat = jnp.pad(w_grid_feat, ((0, 12), (0, 0)))
    row = lambda gain: gain.reshape(1, 512)
    vmem = pl.BlockSpec(memory_space=pltpu.VMEM)
    dma = pltpu.SemaphoreType.DMA
    block = lambda *shape: pltpu.VMEM(shape, BF)
    full, d_terms, mesh_new = pl.pallas_call(
        main_kernel,
        out_shape=[
            jax.ShapeDtypeStruct((6, 2, 4, 4, 4, 16, 128), BF),
            jax.ShapeDtypeStruct((1024, 512), BF),
            jax.ShapeDtypeStruct((64, 512), F32),
        ],
        in_specs=[vmem] * 23,
        out_specs=[vmem] * 3,
        scratch_shapes=reduction_scratch(6)
        + [
            dma((6, 20)),
            dma((6, 20)),
            pltpu.VMEM((6, 512, 512), F32),
            block(9, 64, 512),
            block(9, 16, 256),
            block(9, 64, 512),
            block(9, 64, 512),
            block(64, 512),
            block(9, 64, 512),
            block(64, 512),
            block(128, 512),
            block(64, 512),
            block(64, 512),
            block(1024, 512),
            block(9, 256, 512),
            block(9, 128, 512),
            block(9, 256, 512),
            block(9, 256, 512),
            block(9, 256, 512),
            pltpu.VMEM((9, 256, 1), F32),
            block(9, 256, 512),
            block(9, 64, 512),
            pltpu.VMEM((256, 16), F32),
            dma((6, 9)),
            dma((6, 9)),
        ],
        compiler_params=pltpu.CompilerParams(collective_id=0, has_side_effects=True, vmem_limit_bytes=63 << 20),
        name="step",
    )(
        grid_lat, mesh_lat, g2m_send[0], aux, halo_lists.reshape(1, 64), proc_send, proc_recv, cotangent, w_grid_send,
        w_grid_recv, w_feat, w_grid_out, row(gain_grid), w_node_in, w_node_out, row(gain_node), w_proc_send, w_proc_recv,
        w_proc_out, row(gain_proc), w_upd_in, w_upd_out, row(gain_upd),
    )
    outs = pl.pallas_call(
        finish_kernel,
        grid=(8,),
        out_shape=[jax.ShapeDtypeStruct((512, 512), F32)] * 6
        + [jax.ShapeDtypeStruct((1024, 512), F32), jax.ShapeDtypeStruct((64, 512), F32)],
        in_specs=[
            pl.BlockSpec((6, 1, 1, 4, 4, 16, 128), lambda i: (0, i // 4, lax.rem(i, 4), 0, 0, 0, 0)),
            pl.BlockSpec((128, 512), lambda i: (i, 0)),
            pl.BlockSpec((512, 512), lambda i: (0, 0)),
            pl.BlockSpec((8, 512), lambda i: (i, 0)),
        ],
        out_specs=[pl.BlockSpec((64, 512), lambda i: (i, 0))] * 6
        + [pl.BlockSpec((128, 512), lambda i: (i, 0)), pl.BlockSpec((8, 512), lambda i: (i, 0))],
        name="finish",
    )(full, d_terms, w_grid_send, mesh_new)
    grid_send, grid_recv, grid_out, proc_out, proc_recv_g, proc_send_g, grid_grad, mesh_final = outs
    return mesh_final, grid_grad, grid_send, grid_recv, grid_out, proc_send_g, proc_recv_g, proc_out


def solution(mesh):
    placed = (
        P(("lat", "lon"), None),
        P(("lat", "lon"), None),
        P(("lat", "lon"), None, None),
        P(("lat", "lon"), None, None),
        P(("lat", "lon"), None, None),
        P(("lat", "lon"), None, None),
        P(("lat", "lon"), None),
        P(("lat", "lon"), None),
        P(("lat", "lon"), None),
        P(),
        P(),
        P(),
        P(),
        P(),
        P(),
        P(),
        P(),
        P(),
        P(),
        P(),
        P(),
        P(),
        P(),
        P(),
    )
    return jax.shard_map(
        local,
        mesh=mesh,
        in_specs=placed,
        out_specs=(P(("lat", "lon"), None), P(("lat", "lon"), None), P(), P(), P(), P(), P(), P()),
        check_vma=False,
    )
```

time: 381 us -> 130 us (0.34)
  waiting for transfers between devices: 195 us -> 0 us
  Pallas kernels: 0 us -> 123 us
  matrix products: 48.3 us -> 0 us
  other arithmetic: 43.8 us -> 2.13 us
  starting transfers between devices: 39.5 us -> 0 us
  local copies, waits for them, and re-layouts: 37.7 us -> 3.97 us
  between operations: 15.5 us -> 0.65 us
    psum x1 -> x0, waiting for transfers between devices: 163 us -> none  [local(): lax.psum((grad_grid_send, grad_grid_recv, grad_grid_out, grad_proc_send,...]
    pallas_call x0 -> x2, Pallas kernels: none -> 123 us  [the longest x1 115 us: local(): pl.pallas_call(main_kernel, out_shape=[jax.ShapeDtypeStruct((6, 2, 4, 4,...]
    dot_general x31 -> x0, matrix products: 48.3 us -> none  [the longest x12 21.5 us: inner_rows(): lax.dot_general(matrix_one, matrix_two, (((0,), (0,)), ((), ())), precisi...]
    ppermute x16 -> x0, starting transfers between devices: 39.5 us -> none  [the longest x8 22.4 us: passed_along(): lax.ppermute(value, axis, [(source, source + steps) for source in range(f...]
    ppermute x16 -> x0, waiting for transfers between devices: 32 us -> none  [the longest x8 23 us: passed_along(): lax.ppermute(value, axis, [(source, source + steps) for source in range(f...]
    scatter-add x1 -> x0, other arithmetic: 21.1 us -> none  [local(): jax.ops.segment_sum(back_slots, sender_idx, num_segments=grid_count)]
    gather x5 -> x0, local copies, waits for them, and re-layouts: 18.7 us -> none  [the longest x1 7.51 us: local(): jnp.take(grid_terms, sender_idx, axis=0)]
    unnamed x168 -> x1, local copies, waits for them, and re-layouts: 13.7 us -> 1.31 us
  transfers between devices with their start and end apart: 17 -> 0, of which waited for: 10 -> 0; matrix products, arithmetic and copies ran while one was open for 7% -> 0% of each run, Pallas kernels for 0% -> 0%
where the time goes in v2:
time: 130 us
  Pallas kernels  123 us (95%)
  local copies, waits for them, and re-layouts  3.97 us (3%)
  other arithmetic  2.13 us (2%)
    pallas_call x1, Pallas kernels, local(): pl.pallas_call(main_kernel, out_shape=[jax.ShapeDtypeStruct((6, 2, 4, 4,...  115 us
    pallas_call x1, Pallas kernels, local(): pl.pallas_call(finish_kernel, grid=(8,), out_shape=[jax.ShapeDtypeStruct(...  8.32 us

profile of v2, /device:TPU:1, one launch (start us, length us, event | category | flops | bytes accessed | tf_op | source)
XLA Modules:
  0.0 129.8 jit_solution(17187593664302406366)
XLA Ops:
  0.6 1.3 reshape.44.refs_4_
  1.9 0.1 pad.7.clone
  2.0 0.7 fusion
  2.7 1.3 %copy.40 = s32[1,9,256]{2,1,0:T(8,128)} copy(s32[1,9,256]{2,0,1:T(1,128)} %param.26) | data formatting | bytes 18432
  4.0 1.3 pad.4.refs_10_
  5.3 1.4 %maximum_maximum_fusion.refs_3_ = bf16[9,16,256]{2,1,0:T(8,128)(2,1)} fusion(bf16[9,1,256]{2,1,0:T(2,128)(2,1)S(1)} %copy.34, bf16[9,4,256]{2,1,0:T(4,128)(2,1)} %bitcast.13, bf16[16]{0:T(256)(128)(2,1)S(1)} %pad.7.clone), kind=kLoop, calls=%fused_computation | loop fusion | flops 221184 | bytes 96800 | tf_op jit(solution)/shard_map/concatenate | solution.py:444
  6.7 114.7 %step.1 = (bf16[6,2,4,4,4,16,128]{6,5,4,3,2,1,0:T(8,128)(2,1)}, bf16[1024,512]{1,0:T(8,128)(2,1)}, f32[64,512]{1,0:T(8,128)}) custom-call(bf16[1024,512]{1,0:T(8,128)(2,1)} %refs_0_.1, bf16[64,512]{1,0:T(8,128)(2,1)} %refs_1_.1, s32[9,256]{1,0:T(8,128)} %bitcast.12, bf16[9,16,256]{2,1,0:T(8,128)(2,1)} %maximum_maximum_fusion.refs_3_, ...), custom_call_target="tpu_custom_call" | custom-call | tf_op jit(solution)/shard_map/step/pallas_call | solution.py:450
  121.5 8.3 %finish.1 = (f32[512,512]{1,0:T(8,128)}, f32[512,512]{1,0:T(8,128)}, f32[512,512]{1,0:T(8,128)}, f32[512,512]{1,0:T(8,128)}, f32[512,512]{1,0:T(8,128)}, /*index...) custom-call(bf16[6,2,4,4,4,16,128]{6,5,4,3,2,1,0:T(8,128)(2,1)} %get-tuple-element.19.full, ...), custom_call_target="tpu_custom_call" | custom-call | tf_op jit(solution)/shard_map/finish/pallas_call | solution.py:494
  (2 shorter events, 0.0 us)

commit v3 on v2

v3 whole, which is shorter than its diff:
```python
import functools

import jax
import jax.numpy as jnp
from jax import lax
from jax.experimental import pallas as pl
from jax.experimental.pallas import tpu as pltpu
from jax.sharding import PartitionSpec as P

EPSILON = 1e-05
MESH = pl.DeviceIdType.MESH
ORDERS = ((0, 1, 2), (1, 2, 0), (2, 0, 1))
BF = jnp.bfloat16
F32 = jnp.float32


def mm(a, b):
    return jnp.dot(a, b, preferred_element_type=F32)


def mm_t(a, b):
    return lax.dot_general(a, b, (((0,), (0,)), ((), ())), preferred_element_type=F32)


def mm_nt(a, b):
    return lax.dot_general(a, b, (((1,), (1,)), ((), ())), preferred_element_type=F32)


def tail_forward(pre, weight):
    sig = jax.nn.sigmoid(pre)
    hid = (pre * sig).astype(BF)
    z = mm(hid, weight)
    centre = z - jnp.mean(z, axis=-1, keepdims=True)
    inv = lax.rsqrt(jnp.mean(centre * centre, axis=-1, keepdims=True) + EPSILON)
    return hid, centre * inv, inv, sig + pre * sig * (1.0 - sig)


def tail_backward(grad, gain, zhat, inv, slope, weight):
    u = grad * gain
    m1 = jnp.mean(u, axis=-1, keepdims=True)
    m2 = jnp.mean(u * zhat, axis=-1, keepdims=True)
    dz = (inv * (u - m1 - zhat * m2)).astype(BF)
    return dz, mm_nt(dz, weight) * slope


def coordinates():
    lon = lax.axis_index("lon")
    return (lax.axis_index("lat"), lon // 8, lax.rem(lon // 2, 4), lax.rem(lon, 2))


def device(z, x, y, c):
    return (z, (x * 4 + y) * 2 + c)


def ring_peer(me, dim, step):
    spot = list(me)
    spot[dim] = lax.rem(me[dim] + step, 4)
    return device(*spot)


def core_peer(me):
    return device(me[0], me[1], me[2], 1 - me[3])


def tile_peer(dlat, dlon):
    return (lax.rem(lax.axis_index("lat") + dlat + 4, 4), lax.rem(lax.axis_index("lon") + dlon + 32, 32))


def offset_peer(k, sign):
    return tile_peer(sign * (k // 3 - 1), sign * (lax.rem(k, 3) - 1))


def greet(peers):
    barrier = pltpu.get_barrier_semaphore()
    for peer in peers:
        pl.semaphore_signal(barrier, inc=1, device_id=peer, device_id_type=MESH)
    return barrier, len(peers)


def push(src, dst, send, recv, peer):
    return pltpu.make_async_remote_copy(
        src_ref=src, dst_ref=dst, send_sem=send, recv_sem=recv, device_id=peer, device_id_type=MESH
    )


class Reduction:
    def __init__(self, order, source, bufs, send, recv):
        self.order, self.source = ORDERS[order], source
        self.s0, self.r0, self.s1, self.r1, self.e2, self.e3, self.full = bufs
        self.send, self.recv = send, recv

    def copy(self, slot):
        me = coordinates()
        a, b, c = [me[d] for d in self.order]
        step = (slot - 1) % 3 + 1
        if slot == 0:
            src, dst, peer = self.s0, self.r0, core_peer(me)
        elif slot < 4:
            src, dst = self.s1.at[lax.rem(a + step, 4)], self.r1.at[step - 1]
            peer = ring_peer(me, self.order[0], step)
        elif slot < 7:
            src = dst = self.e2.at[b]
            peer = ring_peer(me, self.order[1], step)
        elif slot < 10:
            src = dst = self.e3.at[c]
            peer = ring_peer(me, self.order[2], step)
        elif slot < 13:
            src = dst = self.full.at[me[3], a]
            peer = ring_peer(me, self.order[0], step)
        else:
            src = dst = self.full.at[me[3]]
            peer = core_peer(me)
        return push(src, dst, self.send.at[slot], self.recv.at[slot], peer)

    def arrive(self, base):
        for k in range(3):
            self.copy(base + k).wait_recv()

    def depart(self, base):
        for step in (1, 3, 2):
            self.copy(base + step - 1).start()

    def begin(self):
        other = pl.multiple_of((1 - coordinates()[3]) * 128, 128)
        self.s0[...] = self.source[pl.ds(other, 128), :].astype(BF)
        self.copy(0).start()

    def stage(self, level):
        me = coordinates()
        a, b, c = [me[d] for d in self.order]
        if level == 0:
            self.copy(0).wait_recv()
            mine = pl.multiple_of(me[3] * 128, 128)
            total = self.source[pl.ds(mine, 128), :] + self.r0[...].astype(F32)
            self.s1[...] = total.astype(BF).reshape(4, 32, 512)
            self.depart(1)
        elif level == 1:
            self.arrive(1)
            total = self.s1[a].astype(F32)
            for k in range(3):
                total = total + self.r1[k].astype(F32)
            self.e2[b] = total.astype(BF)
            self.depart(4)
        elif level == 2:
            self.arrive(4)
            self.e3[c] = total_of(self.e2).astype(BF)
            self.depart(7)
        elif level == 3:
            self.arrive(7)
            self.full[me[3], a] = total_of(self.e3).astype(BF)
            self.depart(10)
        else:
            self.arrive(10)
            self.copy(13).start()

    def finish(self):
        self.copy(13).wait_recv()
        for slot in range(14):
            self.copy(slot).wait_send()


def total_of(ref):
    return (ref[0].astype(F32) + ref[1].astype(F32)) + (ref[2].astype(F32) + ref[3].astype(F32))


def reduction_scratch(count):
    shapes = ((128, 512), (128, 512), (4, 32, 512), (3, 32, 512), (4, 32, 512), (4, 32, 512))
    return [pltpu.VMEM((count,) + s, BF) for s in shapes]


OWN = 4


REMOTE = (1, 7, 3, 5, 0, 6, 2, 8)


def main_kernel(*refs):
    (mesh_lat, send_rows, recv_rows, feat, halo_rows, from_row, to_row, cot, w_feat, gain_grid, gain_node, gain_proc,
     gain_upd) = refs[:13]
    stored = refs[13:24]
    full, d_terms, mesh_out = refs[24:27]
    red = refs[27:33]
    held = refs[33:44]
    (red_send, red_recv, grads, mesh_in, index_in, feat_in, part_out, part_in, dsum_out, dsum_in, halo_out, table, back_out,
     back_in, x_s, slots, hid_s, zhat_s, slope_s, inv_s, dpre_s, drecv_s, cols, ex_send, ex_recv, load) = refs[44:]
    (grid_lat, w_grid_send, w_grid_recv, w_grid_out, w_node_in, w_node_out, w_proc_send, w_proc_recv, w_proc_out, w_upd_in,
     w_upd_out) = held
    loads = [pltpu.make_async_copy(stored[n], held[n], load.at[n]) for n in range(11)]
    for copy in loads[:2]:
        copy.start()
    me = coordinates()
    barrier, greeted = greet([offset_peer(k, 1) for k in range(9) if k != OWN] + [core_peer(me)] + [ring_peer(me, d, s) for d in range(3) for s in (1, 2, 3)])

    def mesh_copy(k):
        return push(mesh_lat, mesh_in.at[k], ex_send.at[0, k], ex_recv.at[0, k], offset_peer(k, -1))

    def index_copy(k):
        return push(recv_rows.at[k], index_in.at[k], ex_send.at[1, k], ex_recv.at[1, k], offset_peer(k, -1))

    def feat_copy(k):
        return push(feat.at[k], feat_in.at[k], ex_send.at[6, k], ex_recv.at[6, k], offset_peer(k, -1))

    def part_copy(k):
        return push(part_out.at[k], part_in.at[k], ex_send.at[2, k], ex_recv.at[2, k], offset_peer(k, 1))

    def dsum_copy(k):
        return push(dsum_out, dsum_in.at[k], ex_send.at[3, k], ex_recv.at[3, k], offset_peer(k, -1))

    ways = ((1, 0), (-1, 0), (0, 1), (0, -1))

    def halo_copy(j):
        return push(halo_out.at[pl.ds(16 * j, 16)], table.at[pl.ds(64 + 16 * j, 16)], ex_send.at[4, j], ex_recv.at[4, j], tile_peer(*ways[j]))

    def back_copy(j):
        dlat, dlon = ways[j]
        return push(back_out.at[pl.ds(16 * j, 16)], back_in.at[pl.ds(16 * j, 16)], ex_send.at[5, j], ex_recv.at[5, j], tile_peer(-dlat, -dlon))

    def each(copy):
        for k in REMOTE:
            copy(k).start()

    loads[0].wait()
    loads[1].wait()
    padded = jnp.concatenate([send_rows[k] for k in range(9)] + [jnp.zeros((7, 256), jnp.int32)], axis=0).astype(F32)
    cols[...] = jnp.transpose(padded)

    def slots_body(k, carry):
        lane = lax.broadcasted_iota(jnp.int32, (256, 16), 1)
        col = jnp.sum(jnp.where(lane == k, cols[...], 0.0), axis=1, keepdims=True).astype(jnp.int32)
        pick = (col == lax.broadcasted_iota(jnp.int32, (256, 1024), 1)).astype(F32).astype(BF)
        x = mm(pick, grid_lat[...]).astype(BF)
        x_s[k] = x
        slots[k] = mm(x, w_grid_send[...]).astype(BF)
        return carry

    lax.fori_loop(0, 3, slots_body, 0)
    pl.semaphore_wait(barrier, greeted)
    each(index_copy)
    each(feat_copy)
    each(mesh_copy)
    for copy in loads[2:]:
        copy.start()
    mesh_in[OWN] = mesh_lat[...]
    index_in[OWN] = recv_rows[OWN]
    feat_in[OWN] = feat[OWN]
    lax.fori_loop(3, 9, slots_body, 0)
    loads[2].wait()
    loads[3].wait()

    def receivers(k):
        return (index_in[k] == lax.broadcasted_iota(jnp.int32, (64, 256), 0)).astype(F32).astype(BF)

    near, far = 5 - 2 * me[3], 3 + 2 * me[3]
    order = (near, far, 1, 7, 0, 6, 2, 8)

    def forward(k):
        if k is not OWN:
            mesh_copy(k).wait_recv()
            index_copy(k).wait_recv()
            feat_copy(k).wait_recv()
        full_terms = mm(mesh_in[k], w_grid_recv[...])
        high = full_terms.astype(BF)
        low = (full_terms - high.astype(F32)).astype(BF)
        rec = receivers(k)
        left = jnp.concatenate([rec, rec, feat_in[k], jnp.zeros((12, 256), BF)], axis=0)
        right = jnp.concatenate([high, low, w_feat[...], jnp.zeros((12, 512), BF)], axis=0)
        pre = slots[k].astype(F32) + mm_t(left, right)
        hid, zhat, inv, slope = tail_forward(pre, w_grid_out[...])
        hid_s[k], zhat_s[k], slope_s[k] = hid, zhat.astype(BF), slope.astype(BF)
        inv_s[k] = inv
        part_out[k] = (mm(rec, zhat.astype(BF)) * gain_grid[...]).astype(BF)
        if k is not OWN:
            part_copy(k).start()

    for k in order + (OWN,):
        forward(k)

    for copy in loads[4:]:
        copy.wait()
    node_pre = mm(mesh_lat[...], w_node_in[:512, :])
    grid_sum = part_out[OWN].astype(F32)
    for k in (3, 5, 1, 7, 0, 6, 2, 8):
        part_copy(k).wait_recv()
        grid_sum = grid_sum + part_in[k].astype(F32)
    node_pre = node_pre + mm(grid_sum.astype(BF), w_node_in[512:, :])
    node_hid, node_zhat, node_inv, node_slope = tail_forward(node_pre, w_node_out[...])
    state = mesh_lat[...].astype(F32) + node_zhat * gain_node[...]
    state_bf = state.astype(BF)
    own_terms = mm(state_bf, w_proc_send[...]).astype(BF)
    spots = lax.broadcasted_iota(jnp.int32, (64, 16), 0)
    lists = [(halo_rows[j : j + 1, :] == spots).astype(F32).astype(BF) for j in range(4)]
    for j in range(4):
        halo_out[pl.ds(16 * j, 16), :] = mm_t(lists[j], own_terms).astype(BF)
        halo_copy(j).start()
    table[:64, :] = own_terms
    p_recv = mm(state_bf, w_proc_recv[...])
    p_high = p_recv.astype(BF)
    p_low = (p_recv - p_high.astype(F32)).astype(BF)
    pick_from = (from_row[...] == lax.broadcasted_iota(jnp.int32, (128, 512), 0)).astype(F32).astype(BF)
    pick_to = (to_row[...] == lax.broadcasted_iota(jnp.int32, (64, 512), 0)).astype(F32).astype(BF)
    upd_pre = mm(state_bf, w_upd_in[:512, :])
    for j in range(4):
        halo_copy(j).wait_recv()
    left = jnp.concatenate([pick_from, pick_to, pick_to], axis=0)
    right = jnp.concatenate([table[...], p_high, p_low], axis=0)
    proc_pre = mm_t(left, right)
    p_hid, p_zhat, p_inv, p_slope = tail_forward(proc_pre, w_proc_out[...])
    proc_sum = mm(pick_to, p_zhat.astype(BF)) * gain_proc[...]
    upd_pre = upd_pre + mm(proc_sum.astype(BF), w_upd_in[512:, :])
    upd_hid, upd_zhat, upd_inv, upd_slope = tail_forward(upd_pre, w_upd_out[...])
    mesh_out[...] = state + upd_zhat * gain_upd[...]
    top = cot[...].astype(F32)
    d_upd = tail_backward(top, gain_upd[...], upd_zhat, upd_inv, upd_slope, w_upd_out[...])[1].astype(BF)
    d_sum = mm_nt(d_upd, w_upd_in[512:, :])
    d_state = top + mm_nt(d_upd, w_upd_in[:512, :])
    d_msg = mm_t(pick_to, d_sum.astype(BF))
    dz, d_pre = tail_backward(d_msg, gain_proc[...], p_zhat, p_inv, p_slope, w_proc_out[...])
    d_pre = d_pre.astype(BF)
    d_table = mm(pick_from, d_pre)
    back_out[...] = d_table[64:, :].astype(BF)
    for j in range(4):
        back_copy(j).start()
    d_recv2 = mm(pick_to, d_pre).astype(BF)
    d_state = d_state + mm_nt(d_recv2, w_proc_recv[...])
    grads[3] = mm_t(p_hid, dz)
    grads[4] = mm_t(state_bf, d_recv2)
    for j in range(4):
        back_copy(j).wait_recv()
    d_own = d_table[:64, :]
    for j in range(4):
        d_own = d_own + mm(lists[j], back_in[pl.ds(16 * j, 16), :])
    d_own = d_own.astype(BF)
    d_state = d_state + mm_nt(d_own, w_proc_send[...])
    d_node = tail_backward(d_state, gain_node[...], node_zhat, node_inv, node_slope, w_node_out[...])[1].astype(BF)
    dsum_out[...] = mm_nt(d_node, w_node_in[512:, :]).astype(BF)
    each(dsum_copy)
    dsum_in[OWN] = dsum_out[...]
    grads[5] = mm_t(state_bf, d_own)
    parts = []
    for n in range(12):
        g, half = n // 2, n % 2
        bufs = [b.at[n] for b in red] + [full.at[g, half]]
        parts.append(Reduction(g % 3, grads.at[g, pl.ds(256 * half, 256)], bufs, red_send.at[n], red_recv.at[n]))
    early = parts[6:]
    for part in early:
        part.begin()

    grads[0] = jnp.zeros((512, 512), F32)
    grads[2] = jnp.zeros((512, 512), F32)
    def backward(k):
        if k is not OWN:
            dsum_copy(k).wait_recv()
        rec = receivers(k)
        grad = mm_t(rec, dsum_in[k])
        zhat = zhat_s[k].astype(F32)
        dz, dpre = tail_backward(grad, gain_grid[...], zhat, inv_s[k], slope_s[k].astype(F32), w_grid_out[...])
        grads[2] += mm_t(hid_s[k], dz)
        dpre = dpre.astype(BF)
        dpre_s[k] = dpre
        grads[0] += mm_t(x_s[k], dpre)
        drecv_s[k] = mm(rec, dpre).astype(BF)

    for n, k in enumerate((OWN,) + order):
        backward(k)
        if n in (1, 5):
            for part in early:
                part.stage(n // 5)
    late = (parts[4], parts[0], parts[5], parts[1], parts[2], parts[3])
    for part in late[:4]:
        part.begin()
    grads[1] = mm_t(mesh_in[...].reshape(576, 512), drecv_s[...].reshape(576, 512))
    for part in late[4:]:
        part.begin()
    every = jnp.concatenate([send_rows[k] for k in range(9)], axis=1)

    def terms_back(i, carry):
        rows = pl.ds(pl.multiple_of(i * 256, 256), 256)
        ids = lax.broadcasted_iota(jnp.int32, (256, 2304), 0) + i * 256
        put = (every == ids).astype(F32).astype(BF)
        d_terms[rows, :] = mm(put, dpre_s[...].reshape(2304, 512)).astype(BF)
        return carry

    def run(group, level):
        for part in group:
            part.stage(level)

    run(late, 0)
    lax.fori_loop(0, 2, terms_back, 0)
    run(early, 2)
    run(late, 1)
    lax.fori_loop(2, 3, terms_back, 0)
    run(early, 3)
    run(late, 2)
    lax.fori_loop(3, 4, terms_back, 0)
    run(early, 4)
    run(late, 3)
    run(late, 4)
    for part in early:
        part.finish()
    for part in late:
        part.finish()
    for k in range(9):
        if k != OWN:
            for copy in (mesh_copy, index_copy, feat_copy, part_copy, dsum_copy):
                copy(k).wait_send()
    for j in range(4):
        halo_copy(j).wait_send()
        back_copy(j).wait_send()


def finish_kernel(full, d_terms, mesh_in, w_grid_send, *refs):
    outs, (weight_v, out_v, grid_v, in_sem, out_sem) = refs[:8], refs[8:]
    load = pltpu.make_async_copy(w_grid_send, weight_v, in_sem)
    load.start()
    done = [pltpu.make_async_copy(mesh_in, outs[7], out_sem.at[10])]
    done[0].start()
    for g in range(6):

        def spread(i, carry, g=g):
            out_v[g, pl.ds(pl.multiple_of(i * 32, 32), 32), :] = full[g, i // 8, lax.rem(i // 4, 2), lax.rem(i, 4)].astype(F32)
            return carry

        lax.fori_loop(0, 16, spread, 0)
        done.append(pltpu.make_async_copy(out_v.at[g], outs[g], out_sem.at[g]))
        done[-1].start()
        if g == 1:
            load.wait()
        if g >= 1 and g < 5:
            rows = pl.ds(256 * (g - 1), 256)
            grid_v[rows, :] = mm_nt(d_terms[rows, :], weight_v[...])
            done.append(pltpu.make_async_copy(grid_v.at[rows], outs[6].at[rows], out_sem.at[5 + g]))
            done[-1].start()
    for copy in done:
        copy.wait()


def local(
    grid_lat,
    mesh_lat,
    g2m_send,
    g2m_recv,
    g2m_feat,
    halo_lists,
    proc_send,
    proc_recv,
    cotangent,
    w_grid_send,
    w_grid_recv,
    w_grid_feat,
    w_grid_out,
    gain_grid,
    w_node_in,
    w_node_out,
    gain_node,
    w_proc_send,
    w_proc_recv,
    w_proc_out,
    gain_proc,
    w_upd_in,
    w_upd_out,
    gain_upd,
):
    feat = g2m_feat[0].reshape(4, 9, 256).transpose(1, 0, 2)
    send_rows = g2m_send.transpose(1, 0, 2)
    recv_rows = g2m_recv.transpose(1, 0, 2)
    row = lambda gain: gain.reshape(1, 512)
    vmem = pl.BlockSpec(memory_space=pltpu.VMEM)
    dma = pltpu.SemaphoreType.DMA
    block = lambda *shape: pltpu.VMEM(shape, BF)
    full, d_terms, mesh_new = pl.pallas_call(
        main_kernel,
        out_shape=[
            pltpu.VMEM((6, 2, 2, 4, 32, 512), BF),
            pltpu.VMEM((1024, 512), BF),
            pltpu.VMEM((64, 512), F32),
        ],
        in_specs=[vmem] * 13 + [pl.BlockSpec(memory_space=pl.ANY)] * 11,
        out_specs=[vmem] * 3,
        scratch_shapes=reduction_scratch(12)
        + [block(1024, 512), block(512, 512), block(512, 512), block(512, 512), block(1024, 512)]
        + [block(512, 512)] * 4
        + [block(1024, 512), block(512, 512)]
        + [
            dma((12, 14)),
            dma((12, 14)),
            pltpu.VMEM((6, 512, 512), F32),
            block(9, 64, 512),
            pltpu.VMEM((9, 1, 256), jnp.int32),
            block(9, 4, 256),
            block(9, 64, 512),
            block(9, 64, 512),
            block(64, 512),
            block(9, 64, 512),
            block(64, 512),
            block(128, 512),
            block(64, 512),
            block(64, 512),
            block(9, 256, 512),
            block(9, 256, 512),
            block(9, 256, 512),
            block(9, 256, 512),
            block(9, 256, 512),
            pltpu.VMEM((9, 256, 1), F32),
            block(9, 256, 512),
            block(9, 64, 512),
            pltpu.VMEM((256, 16), F32),
            dma((7, 9)),
            dma((7, 9)),
            dma((11,)),
        ],
        compiler_params=pltpu.CompilerParams(collective_id=0, has_side_effects=True, vmem_limit_bytes=59 << 20),
        name="step",
    )(
        mesh_lat, send_rows, recv_rows, feat, halo_lists[0], proc_send, proc_recv, cotangent, w_grid_feat, row(gain_grid),
        row(gain_node), row(gain_proc), row(gain_upd), grid_lat, w_grid_send, w_grid_recv, w_grid_out, w_node_in, w_node_out,
        w_proc_send, w_proc_recv, w_proc_out, w_upd_in, w_upd_out,
    )
    outs = pl.pallas_call(
        finish_kernel,
        out_shape=[jax.ShapeDtypeStruct((512, 512), F32)] * 6
        + [jax.ShapeDtypeStruct((1024, 512), F32), jax.ShapeDtypeStruct((64, 512), F32)],
        in_specs=[vmem] * 3 + [pl.BlockSpec(memory_space=pl.ANY)],
        out_specs=[pl.BlockSpec(memory_space=pl.ANY)] * 8,
        scratch_shapes=[
            block(512, 512),
            pltpu.VMEM((6, 512, 512), F32),
            pltpu.VMEM((1024, 512), F32),
            dma,
            dma((11,)),
        ],
        compiler_params=pltpu.CompilerParams(vmem_limit_bytes=40 << 20),
        name="finish",
    )(full, d_terms, mesh_new, w_grid_send)
    grid_send, grid_recv, grid_out, proc_out, proc_recv_g, proc_send_g, grid_grad, mesh_final = outs
    return mesh_final, grid_grad, grid_send, grid_recv, grid_out, proc_send_g, proc_recv_g, proc_out


def solution(mesh):
    placed = (
        P(("lat", "lon"), None),
        P(("lat", "lon"), None),
        P(("lat", "lon"), None, None),
        P(("lat", "lon"), None, None),
        P(("lat", "lon"), None, None),
        P(("lat", "lon"), None, None),
        P(("lat", "lon"), None),
        P(("lat", "lon"), None),
        P(("lat", "lon"), None),
        P(),
        P(),
        P(),
        P(),
        P(),
        P(),
        P(),
        P(),
        P(),
        P(),
        P(),
        P(),
        P(),
        P(),
        P(),
    )
    return jax.shard_map(
        local,
        mesh=mesh,
        in_specs=placed,
        out_specs=(P(("lat", "lon"), None), P(("lat", "lon"), None), P(), P(), P(), P(), P(), P()),
        check_vma=False,
    )
```

time: 130 us -> 87.4 us (0.67)
  Pallas kernels: 123 us -> 86.4 us
  local copies, waits for them, and re-layouts: 3.97 us -> 0.01 us
  other arithmetic: 2.13 us -> 0 us
    pallas_call x2, Pallas kernels: 123 us -> 86.4 us  [the longest x1 82.2 us: local(): pl.pallas_call(main_kernel, out_shape=[pltpu.VMEM((6, 2, 2, 4, 32, 512),...]
    concatenate x1 -> x0, other arithmetic: 1.43 us -> none  [local(): aux = jnp.concatenate([feat, recv, jnp.zeros((9, 11, 256), BF)], axis=1)]
    unnamed x1 -> x2, local copies, waits for them, and re-layouts: 1.31 us -> 0.01 us
where the time goes in v3:
time: 87.4 us; the launch traced here: 87.3 us
  Pallas kernels  86.4 us (99%)
    pallas_call x1, Pallas kernels, local(): pl.pallas_call(main_kernel, out_shape=[pltpu.VMEM((6, 2, 2, 4, 32, 512),...  82.2 us
    pallas_call x1, Pallas kernels, local(): pl.pallas_call(finish_kernel, out_shape=[jax.ShapeDtypeStruct((512, 512),...  4.27 us

profile of v3, /device:TPU:1, one launch (start us, length us, event | category | flops | bytes accessed | tf_op | source)
XLA Modules:
  0.0 87.3 jit_solution(17381072025546906414)
XLA Ops:
  0.6 0.0 copy-start
  0.7 82.2 %step.1 = (bf16[6,2,2,4,32,512]{5,4,3,2,1,0:T(8,128)(2,1)S(1)}, bf16[1024,512]{1,0:T(8,128)(2,1)S(1)}, f32[64,512]{1,0:T(8,128)S(1)}) custom-call(bf16[64,512]{1,0:T(8,128)(2,1)} %refs_0_.1, s32[9,1,256]{2,1,0:T(1,128)} %bitcast.11, s32[9,1,256]{2,1,0:T(1,128)} %bitcast.12, bf16[9,4,256]{2,1,0:T(4,128)(2,1)} %bitcast.10, s32[4,16]{1,0:T(4,128)} %bitcast.13, ...), custom_call_target="tpu_custom_call" | custom-call | tf_op jit(solution)/shard_map/step/pallas_call | solution.py:470
  82.8 0.0 copy-done
  82.8 4.3 %finish.1 = (f32[512,512]{1,0:T(8,128)}, f32[512,512]{1,0:T(8,128)}, f32[512,512]{1,0:T(8,128)}, f32[512,512]{1,0:T(8,128)}, f32[512,512]{1,0:T(8,128)}, /*index...) custom-call(bf16[6,2,2,4,32,512]{5,4,3,2,1,0:T(8,128)(2,1)S(1)} %get-tuple-element.19.full, ...), custom_call_target="tpu_custom_call" | custom-call | tf_op jit(solution)/shard_map/finish/pallas_call | solution.py:518
Async XLA Ops:
  0.6 82.2 %copy-start = (bf16[512,512]{1,0:T(8,128)(2,1)S(1)}, bf16[512,512]{1,0:T(8,128)(2,1)}, u32[]{:S(2)}) copy-start(bf16[512,512]{1,0:T(8,128)(2,1)} %w_grid_send.1) | copy-start | bytes 1572868

commit v4 on v3

--- a/solution.py
+++ b/solution.py
@@ -84,7 +84,8 @@
 
 
 class Reduction:
-    def __init__(self, order, source, bufs, send, recv):
+    def __init__(self, order, source, bufs, send, recv, sized):
+        self.sized = sized
         self.order, self.source = ORDERS[order], source
         self.s0, self.r0, self.s1, self.r1, self.e2, self.e3, self.full = bufs
         self.send, self.recv = send, recv
@@ -110,11 +111,10 @@
         else:
             src = dst = self.full.at[me[3]]
             peer = core_peer(me)
-        return push(src, dst, self.send.at[slot], self.recv.at[slot], peer)
-
-    def arrive(self, base):
-        for k in range(3):
-            self.copy(base + k).wait_recv()
+        return push(src, dst, self.send, self.recv.at[(slot + 2) // 3], peer)
+
+    def wait_for(self, group, ref):
+        push(ref, ref, self.send, self.recv.at[group], core_peer(coordinates())).wait_recv()
 
     def depart(self, base):
         for step in (1, 3, 2):
@@ -129,34 +129,33 @@
         me = coordinates()
         a, b, c = [me[d] for d in self.order]
         if level == 0:
-            self.copy(0).wait_recv()
+            self.wait_for(0, self.r0)
             mine = pl.multiple_of(me[3] * 128, 128)
             total = self.source[pl.ds(mine, 128), :] + self.r0[...].astype(F32)
             self.s1[...] = total.astype(BF).reshape(4, 32, 512)
             self.depart(1)
         elif level == 1:
-            self.arrive(1)
+            self.wait_for(1, self.r1)
             total = self.s1[a].astype(F32)
             for k in range(3):
                 total = total + self.r1[k].astype(F32)
             self.e2[b] = total.astype(BF)
             self.depart(4)
         elif level == 2:
-            self.arrive(4)
+            self.wait_for(2, self.e2.at[pl.ds(0, 3)])
             self.e3[c] = total_of(self.e2).astype(BF)
             self.depart(7)
         elif level == 3:
-            self.arrive(7)
+            self.wait_for(3, self.e3.at[pl.ds(0, 3)])
             self.full[me[3], a] = total_of(self.e3).astype(BF)
             self.depart(10)
         else:
-            self.arrive(10)
+            self.wait_for(4, self.full.at[0, pl.ds(0, 3)])
             self.copy(13).start()
 
     def finish(self):
-        self.copy(13).wait_recv()
-        for slot in range(14):
-            self.copy(slot).wait_send()
+        self.wait_for(5, self.full.at[0])
+        push(self.sized, self.sized, self.send, self.recv.at[0], core_peer(coordinates())).wait_send()
 
 
 def total_of(ref):
@@ -175,52 +174,51 @@
 
 
 def main_kernel(*refs):
-    (mesh_lat, send_rows, recv_rows, feat, halo_rows, from_row, to_row, cot, w_feat, gain_grid, gain_node, gain_proc,
-     gain_upd) = refs[:13]
-    stored = refs[13:24]
-    full, d_terms, mesh_out = refs[24:27]
-    red = refs[27:33]
-    held = refs[33:44]
+    stored, (full, d_terms, mesh_out), red, held = refs[:24], refs[24:27], refs[27:33], refs[33:57]
     (red_send, red_recv, grads, mesh_in, index_in, feat_in, part_out, part_in, dsum_out, dsum_in, halo_out, table, back_out,
-     back_in, x_s, slots, hid_s, zhat_s, slope_s, inv_s, dpre_s, drecv_s, cols, ex_send, ex_recv, load) = refs[44:]
-    (grid_lat, w_grid_send, w_grid_recv, w_grid_out, w_node_in, w_node_out, w_proc_send, w_proc_recv, w_proc_out, w_upd_in,
-     w_upd_out) = held
-    loads = [pltpu.make_async_copy(stored[n], held[n], load.at[n]) for n in range(11)]
-    for copy in loads[:2]:
+     back_in, x_s, slots, hid_s, zhat_s, slope_s, inv_s, dpre_s, drecv_s, cols, ex_send, ex_recv, ex_all, load) = refs[57:]
+    (send_rows, grid_lat, w_grid_send, mesh_lat, recv_rows, feat, w_grid_recv, w_grid_out, w_feat, gain_grid, w_node_in,
+     w_node_out, gain_node, w_proc_send, w_proc_recv, halo_rows, from_row, to_row, w_proc_out, gain_proc, w_upd_in, w_upd_out,
+     gain_upd, cot) = held
+    loads = [pltpu.make_async_copy(stored[n], held[n], load.at[n]) for n in range(24)]
+    for copy in loads[:6]:
         copy.start()
     me = coordinates()
     barrier, greeted = greet([offset_peer(k, 1) for k in range(9) if k != OWN] + [core_peer(me)] + [ring_peer(me, d, s) for d in range(3) for s in (1, 2, 3)])
 
     def mesh_copy(k):
-        return push(mesh_lat, mesh_in.at[k], ex_send.at[0, k], ex_recv.at[0, k], offset_peer(k, -1))
+        return push(mesh_lat, mesh_in.at[k], ex_send.at[0], ex_recv.at[0, k], offset_peer(k, -1))
 
     def index_copy(k):
-        return push(recv_rows.at[k], index_in.at[k], ex_send.at[1, k], ex_recv.at[1, k], offset_peer(k, -1))
+        return push(recv_rows.at[k], index_in.at[k], ex_send.at[1], ex_recv.at[1, k], offset_peer(k, -1))
 
     def feat_copy(k):
-        return push(feat.at[k], feat_in.at[k], ex_send.at[6, k], ex_recv.at[6, k], offset_peer(k, -1))
+        return push(feat.at[k], feat_in.at[k], ex_send.at[2], ex_recv.at[2, k], offset_peer(k, -1))
 
     def part_copy(k):
-        return push(part_out.at[k], part_in.at[k], ex_send.at[2, k], ex_recv.at[2, k], offset_peer(k, 1))
+        return push(part_out.at[k], part_in.at[k], ex_send.at[4], ex_all.at[0], offset_peer(k, 1))
 
     def dsum_copy(k):
-        return push(dsum_out, dsum_in.at[k], ex_send.at[3, k], ex_recv.at[3, k], offset_peer(k, -1))
+        return push(dsum_out, dsum_in.at[k], ex_send.at[3], ex_recv.at[3, k], offset_peer(k, -1))
 
     ways = ((1, 0), (-1, 0), (0, 1), (0, -1))
 
     def halo_copy(j):
-        return push(halo_out.at[pl.ds(16 * j, 16)], table.at[pl.ds(64 + 16 * j, 16)], ex_send.at[4, j], ex_recv.at[4, j], tile_peer(*ways[j]))
+        return push(halo_out.at[pl.ds(16 * j, 16)], table.at[pl.ds(64 + 16 * j, 16)], ex_send.at[5], ex_all.at[1], tile_peer(*ways[j]))
 
     def back_copy(j):
         dlat, dlon = ways[j]
-        return push(back_out.at[pl.ds(16 * j, 16)], back_in.at[pl.ds(16 * j, 16)], ex_send.at[5, j], ex_recv.at[5, j], tile_peer(-dlat, -dlon))
+        return push(back_out.at[pl.ds(16 * j, 16)], back_in.at[pl.ds(16 * j, 16)], ex_send.at[6], ex_all.at[2], tile_peer(-dlat, -dlon))
+
+    def landed(ref, n):
+        push(ref, ref, ex_send.at[0], ex_all.at[n], core_peer(me)).wait_recv()
 
     def each(copy):
         for k in REMOTE:
             copy(k).start()
 
-    loads[0].wait()
-    loads[1].wait()
+    for copy in loads[:3]:
+        copy.wait()
     padded = jnp.concatenate([send_rows[k] for k in range(9)] + [jnp.zeros((7, 256), jnp.int32)], axis=0).astype(F32)
     cols[...] = jnp.transpose(padded)
 
@@ -234,18 +232,20 @@
         return carry
 
     lax.fori_loop(0, 3, slots_body, 0)
+    for copy in loads[3:6]:
+        copy.wait()
     pl.semaphore_wait(barrier, greeted)
     each(index_copy)
     each(feat_copy)
     each(mesh_copy)
-    for copy in loads[2:]:
+    for copy in loads[6:]:
         copy.start()
     mesh_in[OWN] = mesh_lat[...]
     index_in[OWN] = recv_rows[OWN]
     feat_in[OWN] = feat[OWN]
     lax.fori_loop(3, 9, slots_body, 0)
-    loads[2].wait()
-    loads[3].wait()
+    for copy in loads[6:10]:
+        copy.wait()
 
     def receivers(k):
         return (index_in[k] == lax.broadcasted_iota(jnp.int32, (64, 256), 0)).astype(F32).astype(BF)
@@ -275,12 +275,12 @@
     for k in order + (OWN,):
         forward(k)
 
-    for copy in loads[4:]:
+    for copy in loads[10:]:
         copy.wait()
     node_pre = mm(mesh_lat[...], w_node_in[:512, :])
     grid_sum = part_out[OWN].astype(F32)
-    for k in (3, 5, 1, 7, 0, 6, 2, 8):
-        part_copy(k).wait_recv()
+    landed(part_in.at[pl.ds(0, 8)], 0)
+    for k in REMOTE:
         grid_sum = grid_sum + part_in[k].astype(F32)
     node_pre = node_pre + mm(grid_sum.astype(BF), w_node_in[512:, :])
     node_hid, node_zhat, node_inv, node_slope = tail_forward(node_pre, w_node_out[...])
@@ -299,8 +299,7 @@
     pick_from = (from_row[...] == lax.broadcasted_iota(jnp.int32, (128, 512), 0)).astype(F32).astype(BF)
     pick_to = (to_row[...] == lax.broadcasted_iota(jnp.int32, (64, 512), 0)).astype(F32).astype(BF)
     upd_pre = mm(state_bf, w_upd_in[:512, :])
-    for j in range(4):
-        halo_copy(j).wait_recv()
+    landed(table.at[pl.ds(64, 64)], 1)
     left = jnp.concatenate([pick_from, pick_to, pick_to], axis=0)
     right = jnp.concatenate([table[...], p_high, p_low], axis=0)
     proc_pre = mm_t(left, right)
@@ -324,8 +323,7 @@
     d_state = d_state + mm_nt(d_recv2, w_proc_recv[...])
     grads[3] = mm_t(p_hid, dz)
     grads[4] = mm_t(state_bf, d_recv2)
-    for j in range(4):
-        back_copy(j).wait_recv()
+    landed(back_in, 2)
     d_own = d_table[:64, :]
     for j in range(4):
         d_own = d_own + mm(lists[j], back_in[pl.ds(16 * j, 16), :])
@@ -340,7 +338,7 @@
     for n in range(12):
         g, half = n // 2, n % 2
         bufs = [b.at[n] for b in red] + [full.at[g, half]]
-        parts.append(Reduction(g % 3, grads.at[g, pl.ds(256 * half, 256)], bufs, red_send.at[n], red_recv.at[n]))
+        parts.append(Reduction(g % 3, grads.at[g, pl.ds(256 * half, 256)], bufs, red_send.at[n], red_recv.at[n], red[2].at[pl.ds(0, 5)]))
     early = parts[6:]
     for part in early:
         part.begin()
@@ -399,13 +397,9 @@
         part.finish()
     for part in late:
         part.finish()
-    for k in range(9):
-        if k != OWN:
-            for copy in (mesh_copy, index_copy, feat_copy, part_copy, dsum_copy):
-                copy(k).wait_send()
-    for j in range(4):
-        halo_copy(j).wait_send()
-        back_copy(j).wait_send()
+    sent = (mesh_in, index_in, feat_in, dsum_in, part_in)
+    for n, ref in enumerate([r.at[pl.ds(0, 8)] for r in sent] + [table.at[pl.ds(0, 64)], back_in]):
+        push(ref, ref, ex_send.at[n], ex_all.at[0], core_peer(me)).wait_send()
 
 
 def finish_kernel(full, d_terms, mesh_in, w_grid_send, *refs):
@@ -467,6 +461,11 @@
     vmem = pl.BlockSpec(memory_space=pltpu.VMEM)
     dma = pltpu.SemaphoreType.DMA
     block = lambda *shape: pltpu.VMEM(shape, BF)
+    given = (
+        send_rows, grid_lat, w_grid_send, mesh_lat, recv_rows, feat, w_grid_recv, w_grid_out, w_grid_feat, row(gain_grid),
+        w_node_in, w_node_out, row(gain_node), w_proc_send, w_proc_recv, halo_lists[0], proc_send, proc_recv, w_proc_out,
+        row(gain_proc), w_upd_in, w_upd_out, row(gain_upd), cotangent,
+    )
     full, d_terms, mesh_new = pl.pallas_call(
         main_kernel,
         out_shape=[
@@ -474,15 +473,13 @@
             pltpu.VMEM((1024, 512), BF),
             pltpu.VMEM((64, 512), F32),
         ],
-        in_specs=[vmem] * 13 + [pl.BlockSpec(memory_space=pl.ANY)] * 11,
+        in_specs=[pl.BlockSpec(memory_space=pl.ANY)] * 24,
         out_specs=[vmem] * 3,
         scratch_shapes=reduction_scratch(12)
-        + [block(1024, 512), block(512, 512), block(512, 512), block(512, 512), block(1024, 512)]
-        + [block(512, 512)] * 4
-        + [block(1024, 512), block(512, 512)]
+        + [pltpu.VMEM(value.shape, value.dtype) for value in given]
         + [
-            dma((12, 14)),
-            dma((12, 14)),
+            dma((12,)),
+            dma((12, 6)),
             pltpu.VMEM((6, 512, 512), F32),
             block(9, 64, 512),
             pltpu.VMEM((9, 1, 256), jnp.int32),
@@ -504,17 +501,14 @@
             block(9, 256, 512),
             block(9, 64, 512),
             pltpu.VMEM((256, 16), F32),
-            dma((7, 9)),
-            dma((7, 9)),
-            dma((11,)),
+            dma((7,)),
+            dma((4, 9)),
+            dma((3,)),
+            dma((24,)),
         ],
         compiler_params=pltpu.CompilerParams(collective_id=0, has_side_effects=True, vmem_limit_bytes=59 << 20),
         name="step",
-    )(
-        mesh_lat, send_rows, recv_rows, feat, halo_lists[0], proc_send, proc_recv, cotangent, w_grid_feat, row(gain_grid),
-        row(gain_node), row(gain_proc), row(gain_upd), grid_lat, w_grid_send, w_grid_recv, w_grid_out, w_node_in, w_node_out,
-        w_proc_send, w_proc_recv, w_proc_out, w_upd_in, w_upd_out,
-    )
+    )(*given)
     outs = pl.pallas_call(
         finish_kernel,
         out_shape=[jax.ShapeDtypeStruct((512, 512), F32)] * 6

time: 87.4 us -> 83.6 us (0.957)
  Pallas kernels: 86.4 us -> 82.7 us
    pallas_call x1, Pallas kernels: 82.2 us -> 78.4 us  [local(): pl.pallas_call(main_kernel, out_shape=[pltpu.VMEM((6, 2, 2, 4, 32, 512),...]
where the time goes in v4:
time: 83.6 us; the launch traced here: 83.5 us
  Pallas kernels  82.7 us (99%)
    pallas_call x1, Pallas kernels, local(): pl.pallas_call(main_kernel, out_shape=[pltpu.VMEM((6, 2, 2, 4, 32, 512),...  78.4 us
    pallas_call x1, Pallas kernels, local(): pl.pallas_call(finish_kernel, out_shape=[jax.ShapeDtypeStruct((512, 512),...  4.27 us

profile of v4, /device:TPU:1, one launch (start us, length us, event | category | flops | bytes accessed | tf_op | source)
XLA Modules:
  0.0 83.5 jit_solution(8325546935323912868)
XLA Ops:
  0.6 0.0 copy-start
  0.7 78.4 %step.1 = (bf16[6,2,2,4,32,512]{5,4,3,2,1,0:T(8,128)(2,1)S(1)}, bf16[1024,512]{1,0:T(8,128)(2,1)S(1)}, f32[64,512]{1,0:T(8,128)S(1)}) custom-call(s32[9,1,256]{2,1,0:T(1,128)} %bitcast.11, bf16[1024,512]{1,0:T(8,128)(2,1)} %refs_1_.1, bf16[512,512]{1,0:T(8,128)(2,1)} %w_grid_send.1, bf16[64,512]{1,0:T(8,128)(2,1)} %refs_3_.1, s32[9,1,256]{2,1,0:T(1,128)} %bitcast.12, ...), custom_call_target="tpu_custom_call" | custom-call | tf_op jit(solution)/shard_map/step/pallas_call | solution.py:469
  79.0 0.0 copy-done
  79.1 4.3 %finish.1 = (f32[512,512]{1,0:T(8,128)}, f32[512,512]{1,0:T(8,128)}, f32[512,512]{1,0:T(8,128)}, f32[512,512]{1,0:T(8,128)}, f32[512,512]{1,0:T(8,128)}, /*index...) custom-call(bf16[6,2,2,4,32,512]{5,4,3,2,1,0:T(8,128)(2,1)S(1)} %get-tuple-element.19.full, ...), custom_call_target="tpu_custom_call" | custom-call | tf_op jit(solution)/shard_map/finish/pallas_call | solution.py:512
Async XLA Ops:
  0.6 78.4 %copy-start = (bf16[512,512]{1,0:T(8,128)(2,1)S(1)}, bf16[512,512]{1,0:T(8,128)(2,1)}, u32[]{:S(2)}) copy-start(bf16[512,512]{1,0:T(8,128)(2,1)} %w_grid_send.1) | copy-start | bytes 1572868

commit v5 on v4

--- a/solution.py
+++ b/solution.py
@@ -360,9 +360,9 @@
 
     for n, k in enumerate((OWN,) + order):
         backward(k)
-        if n in (1, 5):
+        if n == 3:
             for part in early:
-                part.stage(n // 5)
+                part.stage(0)
     late = (parts[4], parts[0], parts[5], parts[1], parts[2], parts[3])
     for part in late[:4]:
         part.begin()
@@ -383,6 +383,7 @@
             part.stage(level)
 
     run(late, 0)
+    run(early, 1)
     lax.fori_loop(0, 2, terms_back, 0)
     run(early, 2)
     run(late, 1)

time: 83.6 us -> 87.4 us (1.045)
  Pallas kernels: 82.7 us -> 86.5 us
    pallas_call x1, Pallas kernels: 78.4 us -> 82.2 us  [local(): pl.pallas_call(main_kernel, out_shape=[pltpu.VMEM((6, 2, 2, 4, 32, 512),...]
where the time goes in v5:
time: 87.4 us; the launch traced here: 87.3 us
  Pallas kernels  86.5 us (99%)
    pallas_call x1, Pallas kernels, local(): pl.pallas_call(main_kernel, out_shape=[pltpu.VMEM((6, 2, 2, 4, 32, 512),...  82.2 us
    pallas_call x1, Pallas kernels, local(): pl.pallas_call(finish_kernel, out_shape=[jax.ShapeDtypeStruct((512, 512),...  4.27 us

profile of v5, /device:TPU:1, one launch (start us, length us, event | category | flops | bytes accessed | tf_op | source)
XLA Modules:
  0.0 87.3 jit_solution(14265267710035464268)
XLA Ops:
  0.6 0.0 copy-start
  0.7 82.2 %step.1 = (bf16[6,2,2,4,32,512]{5,4,3,2,1,0:T(8,128)(2,1)S(1)}, bf16[1024,512]{1,0:T(8,128)(2,1)S(1)}, f32[64,512]{1,0:T(8,128)S(1)}) custom-call(s32[9,1,256]{2,1,0:T(1,128)} %bitcast.11, bf16[1024,512]{1,0:T(8,128)(2,1)} %refs_1_.1, bf16[512,512]{1,0:T(8,128)(2,1)} %w_grid_send.1, bf16[64,512]{1,0:T(8,128)(2,1)} %refs_3_.1, s32[9,1,256]{2,1,0:T(1,128)} %bitcast.12, ...), custom_call_target="tpu_custom_call" | custom-call | tf_op jit(solution)/shard_map/step/pallas_call | solution.py:470
  82.9 0.0 copy-done
  82.9 4.3 %finish.1 = (f32[512,512]{1,0:T(8,128)}, f32[512,512]{1,0:T(8,128)}, f32[512,512]{1,0:T(8,128)}, f32[512,512]{1,0:T(8,128)}, f32[512,512]{1,0:T(8,128)}, /*index...) custom-call(bf16[6,2,2,4,32,512]{5,4,3,2,1,0:T(8,128)(2,1)S(1)} %get-tuple-element.19.full, ...), custom_call_target="tpu_custom_call" | custom-call | tf_op jit(solution)/shard_map/finish/pallas_call | solution.py:513
Async XLA Ops:
  0.6 82.2 %copy-start = (bf16[512,512]{1,0:T(8,128)(2,1)S(1)}, bf16[512,512]{1,0:T(8,128)(2,1)}, u32[]{:S(2)}) copy-start(bf16[512,512]{1,0:T(8,128)(2,1)} %w_grid_send.1) | copy-start | bytes 1572868
